TPU v7x, 256 devices: a whole 4x4x8 slice. The times are simulated.
256 devices in a mesh: seq: 64 (over y, z, core), head: 4 (over x).
Axes of the slice: x: 4, y: 4, z: 8, core: 2. Of those that a mesh axis runs over, the one named last changes fastest.
Arguments:
- queries: bfloat16 [32768, 8192], P('seq', 'head'), may hold values from -6 to 6
- keys: bfloat16 [32768, 8192], P('seq', 'head'), may hold values from -0.52734375 to 0.52734375
- values: bfloat16 [32768, 8192], P('seq', 'head'), may hold values from -6 to 6
- suffix_keys: bfloat16 [256, 128, 8192], P('seq', None, 'head'), may hold values from -0.52734375 to 0.52734375
- suffix_values: bfloat16 [256, 128, 8192], P('seq', None, 'head'), may hold values from -6 to 6
- suffix_lengths: int32 [256], P('seq'), may hold values from 1 to 128
- step_queries: bfloat16 [2, 256, 8192], P(None, 'seq', 'head'), may hold values from -6 to 6
- step_keys: bfloat16 [2, 256, 8192], P(None, 'seq', 'head'), may hold values from -0.52734375 to 0.52734375
- step_values: bfloat16 [2, 256, 8192], P(None, 'seq', 'head'), may hold values from -6 to 6
- norm_gain: float32 [8192], P('head'), may hold values from 0.1 to 1.9
Outputs:
- prompt_out: bfloat16 [32768, 8192], P('seq', 'head')
- decoded: bfloat16 [2, 256, 8192], P(None, 'seq', 'head')
All inputs are finite; a program needn't handle non-finite values.
Results may differ from a plain program's by a relative error of at most 0.005.
Values sent between devices are 32-bit elements; how exact they have to be, the bound alone decides.
A program may use at most 128 MiB of HBM per device.

v0:
```python
import jax
import jax.numpy as jnp
from jax import lax
from jax.sharding import Mesh
from jax.sharding import PartitionSpec as P

HEAD_DIM = 128
SEQ = ("seq_0", "seq_1", "seq_2")


HIGHEST_PREC = lax.Precision.HIGHEST


def neutral_like(array, identity):
    return jnp.zeros_like(array) + jnp.asarray(identity, array.dtype)


def entering(array, axes, combine, identity):
    before = start = neutral_like(array, identity)
    subtotal = array
    for axis in reversed(axes):
        peers, position = (lax.axis_size(axis), lax.axis_index(axis))
        pieces = lax.all_gather(subtotal, axis)
        inside, subtotal = (start, start)
        for k in range(peers):
            passed = k < position
            subtotal = combine(subtotal, pieces[k])
            inside = jnp.where(passed, subtotal, inside)
        before = combine(inside, before)
    return before


def filled_up(lines, peers):
    spare = -lines.shape[0] % peers
    if not spare:
        return lines
    return jnp.concatenate([lines, jnp.zeros((spare, *lines.shape[1:]), lines.dtype)])


def copy_for_each(array, axis):
    peers = lax.axis_size(axis)
    return lax.all_to_all(
        jnp.broadcast_to(array[None], (peers, *array.shape)), axis, 0, 0, tiled=True
    )


def laid_out(pieces, dim):
    shape = list(pieces.shape[1:])
    shape[dim] *= pieces.shape[0]
    return jnp.moveaxis(pieces, 0, dim).reshape(shape)


def gathered_by_axis(array, axes, dim):
    far, near = axes
    first = copy_for_each(array, far)
    pieces = jnp.swapaxes(copy_for_each(first, near), 0, 1)
    return laid_out(pieces.reshape(-1, *array.shape), dim)


def split_up(array, dim, peers):
    before, after = (array.shape[:dim], array.shape[dim + 1 :])
    return jnp.moveaxis(array.reshape(*before, peers, -1, *after), dim, 0)


def summed_on_arrival(array, axis, dim):
    pieces = split_up(array, dim, lax.axis_size(axis))
    arrived = lax.all_to_all(pieces, axis, split_axis=0, concat_axis=0, tiled=True)
    return arrived.sum(axis=0)


def summed_rows(array, axes, dim):
    far, near = axes
    pieces = split_up(array, dim, lax.axis_size(far))
    nearer = summed_on_arrival(pieces, near, dim + 1)
    arrived = lax.all_to_all(nearer, far, split_axis=0, concat_axis=0, tiled=True)
    return arrived.sum(axis=0)


def nested_sum(array, axes):
    lines = array.reshape(-1, array.shape[-1])
    padded = filled_up(lines, lax.axis_size(axes[0]) * lax.axis_size(axes[1]))
    whole = gathered_by_axis(summed_rows(padded, axes, 0), axes, 0)
    return lax.slice_in_dim(whole, 0, len(lines)).reshape(array.shape)


def over_copies(array, axis):
    everything = copy_for_each(array, axis)
    return jnp.sum(everything, axis=0)


def add_states(earlier, later):
    return earlier + later


def on_device(
    queries,
    keys,
    values,
    suffix_keys,
    suffix_values,
    suffix_lengths,
    step_queries,
    step_keys,
    step_values,
    norm_gain,
):
    rows_here = queries.shape[0]
    heads_here = queries.shape[1] // HEAD_DIM
    block_queries = queries.reshape(rows_here, heads_here, HEAD_DIM)
    block_keys = keys.reshape(rows_here, heads_here, HEAD_DIM)
    block_values = values.reshape(rows_here, heads_here, HEAD_DIM)
    own_state = jnp.einsum(
        "chd,che->hde", block_keys, block_values, preferred_element_type=jnp.float32
    )
    prior = entering(own_state, SEQ, add_states, jnp.zeros_like(own_state))
    final = nested_sum(own_state, (("seq_0", "seq_1"), "seq_2"))
    positions = lax.iota(jnp.int32, rows_here)
    causal = positions[None, :] <= positions[:, None]
    scores = jnp.einsum(
        "chd,shd->hcs", block_queries, block_keys, preferred_element_type=jnp.float32
    )
    scores = jnp.where(causal[None], scores, 0.0).astype(jnp.bfloat16)
    intra = jnp.einsum("hcs,she->che", scores, block_values, preferred_element_type=jnp.float32)
    inter = jnp.einsum(
        "chd,hde->che",
        block_queries,
        prior.astype(jnp.bfloat16),
        preferred_element_type=jnp.float32,
    )
    attended = (intra + inter).reshape(rows_here, heads_here * HEAD_DIM)
    total_sq = over_copies(jnp.sum(attended * attended, axis=1), "head")
    width_all = heads_here * HEAD_DIM * lax.axis_size("head")
    scale_rows = lax.rsqrt(total_sq / width_all + 1e-06)
    prompt_out = (attended * scale_rows[:, None] * norm_gain).astype(jnp.bfloat16)
    samples_here = suffix_keys.shape[0]
    suffix_len = suffix_keys.shape[1]
    live = (lax.iota(jnp.int32, suffix_len)[None, :] < suffix_lengths[:, None]).astype(jnp.bfloat16)
    masked_keys = (suffix_keys * live[:, :, None]).reshape(
        samples_here, suffix_len, heads_here, HEAD_DIM
    )
    suffix_vals = suffix_values.reshape(samples_here, suffix_len, heads_here, HEAD_DIM)
    state = final[None] + jnp.einsum(
        "bjhd,bjhe->bhde", masked_keys, suffix_vals, preferred_element_type=jnp.float32
    )
    outputs = []
    for step in range(step_queries.shape[0]):
        new_keys = step_keys[step].reshape(samples_here, heads_here, HEAD_DIM)
        new_vals = step_values[step].reshape(samples_here, heads_here, HEAD_DIM)
        new_query = (
            step_queries[step].reshape(samples_here, heads_here, HEAD_DIM).astype(jnp.float32)
        )
        state = state + jnp.einsum(
            "bhd,bhe->bhde", new_keys, new_vals, preferred_element_type=jnp.float32
        )
        raw = jnp.einsum("bhd,bhde->bhe", new_query, state, precision=HIGHEST_PREC)
        outputs.append(raw.reshape(samples_here, heads_here * HEAD_DIM))
    stacked = jnp.stack(outputs)
    step_sq = over_copies(jnp.sum(stacked * stacked, axis=2), "head")
    scale_steps = lax.rsqrt(step_sq / width_all + 1e-06)
    decoded = (stacked * scale_steps[:, :, None] * norm_gain).astype(jnp.bfloat16)
    return (prompt_out, decoded)


def solution(mesh):
    finer = Mesh(
        mesh.devices.reshape(4, 8, 2, mesh.shape["head"]), ("seq_0", "seq_1", "seq_2", "head")
    )
    return jax.shard_map(
        on_device,
        mesh=finer,
        in_specs=(
            P(SEQ, "head"),
            P(SEQ, "head"),
            P(SEQ, "head"),
            P(SEQ, None, "head"),
            P(SEQ, None, "head"),
            P(SEQ),
            P(None, SEQ, "head"),
            P(None, SEQ, "head"),
            P(None, SEQ, "head"),
            P("head"),
        ),
        out_specs=(P(SEQ, "head"), P(None, SEQ, "head")),
        check_vma=False,
    )
```

profile of v0, /device:TPU:1, one launch (start us, length us, event | category | flops | bytes accessed | tf_op | source)
XLA Modules:
  0.0 244.8 jit_solution(5789952279692240009)
XLA Ops:
  7.2 4.1 %copy.75 = bf16[512,2048]{0,1:T(8,128)(2,1)} copy(bf16[512,2048]{1,0:T(8,128)(2,1)} %param.11) | data formatting | bytes 4194304 | tf_op jit(solution)/shard_map/reshape | solution.py:110
  11.3 4.0 %fusion.9 = f32[16,128,128]{2,1,0:T(8,128)} fusion(bf16[512,16,128]{0,2,1:T(8,128)(2,1)} %bitcast.135, bf16[512,2048]{1,0:T(8,128)(2,1)} %param.12), kind=kOutput, calls=%fused_computation.14 | convolution fusion | flops 268435456 | bytes 5242880 | tf_op jit(solution)/shard_map/chd,che->hde/dot_general | solution.py:112
  15.4 20.5 %all-gather.8.cloned.1.call-done = f32[32,128,128]{2,1,0:T(8,128)} async-done(((f32[16,128,128]{2,1,0:T(8,128)}), f32[32,128,128]{2,1,0:T(8,128)}) %all-gather.8.cloned.1.call-update) | async-done | bytes 2097168 | tf_op jit(solution)/shard_map/all_gather | solution.py:23
  35.9 2.7 %slice_add_fusion.8 = f32[16,128,128]{2,1,0:T(8,128)} fusion(f32[32,128,128]{2,1,0:T(8,128)} %all-gather.8.cloned.1.call-done), kind=kLoop, calls=%fused_computation.46 | loop fusion | flops 262144 | bytes 3145728 | tf_op jit(solution)/shard_map/add | solution.py:92
  38.7 94.6 %all-gather.10.cloned.1.call-done = f32[128,128,128]{2,1,0:T(8,128)} async-done(((f32[16,128,128]{2,1,0:T(8,128)}), f32[128,128,128]{2,1,0:T(8,128)}) %all-gather.10.cloned.1.call-update) | async-done | bytes 8388624 | tf_op jit(solution)/shard_map/all_gather | solution.py:23
  133.3 5.7 %fusion.30 = (f32[1,16,128,128]{3,2,1,0:T(8,128)}, f32[16,128,128]{2,1,0:T(8,128)}) fusion(f32[128,128,128]{2,1,0:T(8,128)} %all-gather.10.cloned.1.call-done), kind=kLoop, calls=%fused_computation.37 | loop fusion | flops 1835008 | bytes 10485760 | tf_op jit(solution)/shard_map/add | solution.py:92
  139.1 5.0 %all_to_all.31 = f32[2,32,32,128]{3,2,1,0:T(8,128)S(1)} all-to-all(f32[2,32,32,128]{3,2,1,0:T(8,128)S(1)} %bitcast.139), channel_id=1, replica_groups=mesh['seq_0'=4,'seq_1'=8,'seq_2'=2,'head'=4] {'seq_2'}, dimensions={0} | all-to-all | bytes 2097152 | tf_op jit(solution)/shard_map/all_to_all | solution.py:67
  145.1 6.9 %all-to-all-start.2 = ((f32[32,32,128]{2,1,0:T(8,128)}), f32[32,32,128]{2,1,0:T(8,128)S(1)}, u32[]{:S(2)}, u32[]{:S(2)}) async-start(f32[32,32,128]{2,1,0:T(8,128)} %reduce_sum.56), calls=%async_computation.2 | async-start | bytes 1048576 | tf_op jit(solution)/shard_map/all_to_all | solution.py:75
  152.1 3.3 %broadcast_multiply_fusion = bf16[4,128,2048]{2,1,0:T(8,128)(2,1)} fusion(bf16[4,128,2048]{2,1,0:T(8,128)(2,1)} %param.13, bf16[4,128]{1,0:T(4,128)(2,1)S(1)} %fusion.53), kind=kLoop, calls=%fused_computation.52 | loop fusion | flops 1048576 | bytes 4195328 | tf_op jit(solution)/shard_map/mul | solution.py:138
  155.5 4.0 %copy.72 = bf16[4,128,2048]{1,2,0:T(8,128)(2,1)} copy(bf16[4,128,2048]{2,1,0:T(8,128)(2,1)} %broadcast_multiply_fusion) | data formatting | bytes 4194304 | tf_op jit(solution)/shard_map/reshape | solution.py:138
  159.6 4.9 %fusion.5 = f32[4,16,128,128]{3,2,1,0:T(8,128)} fusion(bf16[4,128,16,128]{1,3,2,0:T(8,128)(2,1)} %bitcast.137, bf16[4,128,2048]{2,1,0:T(8,128)(2,1)} %param.14), kind=kOutput, calls=%fused_computation.10 | convolution fusion | flops 268435456 | bytes 8388608 | tf_op jit(solution)/shard_map/bjhd,bjhe->bhde/dot_general | solution.py:142
  164.5 1.7 all-to-all-done.2
  167.1 8.1 %all-to-all-start.3 = ((f32[32,32,128]{2,1,0:T(8,128)}), f32[32,32,128]{2,1,0:T(8,128)S(1)}, u32[]{:S(2)}, u32[]{:S(2)}) async-start(f32[32,32,128]{2,1,0:T(8,128)} %broadcast_in_dim.26), calls=%async_computation.3 | async-start | bytes 1048576 | tf_op jit(solution)/shard_map/all_to_all | solution.py:42
  175.2 9.3 %fusion.4 = f32[16,512,128]{1,2,0:T(8,128)} fusion(bf16[512,16,128]{0,2,1:T(8,128)(2,1)} %bitcast.136, pred[512,512]{1,0:T(8,128)(4,1)S(1)} %iota_compare_fusion, bf16[512,2048]{1,0:T(8,128)(2,1)} %param.12, bf16[512,2048]{1,0:T(8,128)(2,1)S(1)} %copy-done), kind=kOutput, calls=%fused_computation.9 | convolution fusion | flops 2155872256 | bytes 10747904 | tf_op jit(solution)/shard_map/hcs,she->che/dot_general | solution.py:123
  184.5 4.9 %all-to-all-done.3 = f32[32,32,128]{2,1,0:T(8,128)S(1)} async-done(((f32[32,32,128]{2,1,0:T(8,128)}), f32[32,32,128]{2,1,0:T(8,128)S(1)}, u32[]{:S(2)}, u32[]{:S(2)}) %all-to-all-start.3) | async-done | bytes 524320 | tf_op jit(solution)/shard_map/all_to_all | solution.py:42
  189.5 8.1 %all_to_all.32 = f32[2,32,32,128]{3,2,1,0:T(8,128)S(1)} all-to-all(f32[2,32,32,128]{3,2,1,0:T(8,128)S(1)} %broadcast_in_dim.27), channel_id=1, replica_groups=mesh['seq_0'=4,'seq_1'=8,'seq_2'=2,'head'=4] {'seq_2'}, dimensions={0} | all-to-all | bytes 2097152 | tf_op jit(solution)/shard_map/all_to_all | solution.py:42
  197.8 2.7 %fusion.3 = f32[4,16,1,128]{3,2,1,0:T(1,128)S(1)} fusion(bf16[4,16,128,1]{2,3,1,0:T(2,128)(2,1)S(1)} %reshape.192, f32[4,16,128,128]{3,2,1,0:T(8,128)S(1)} %copy-done.1, f32[4,16,128]{2,1,0:T(8,128)S(1)} %get-tuple-element.13, f32[4,16,128]{2,1,0:T(8,128)S(1)} %get-tuple-element.15, f32[16,128,128]{2,1,0:T(8,128)S(1)} %bitcast.140), kind=kOutput, calls=%fused_computation.8 | convolution fusion | flops 15728640 | bytes 5357568 | tf_op jit(solution)/shard_map/bhd,bhde->bhe/dot_general | solution.py:155
  200.5 5.4 %fusion = f32[4,16,1,128]{3,2,1,0:T(1,128)S(1)} fusion(bf16[4,16,128,1]{2,3,1,0:T(2,128)(2,1)S(1)} %reshape.194, f32[4,16,128,128]{3,2,1,0:T(8,128)} %fusion.5, f32[4,16,128]{2,1,0:T(8,128)S(1)} %get-tuple-element.12, f32[4,16,128]{2,1,0:T(8,128)S(1)} %get-tuple-element.14, f32[4,16,128]{2,1,0:T(8,128)S(1)} %get-tuple-element.13, ...), kind=kOutput, calls=%fused_computation.2 | convolution fusion | flops 17825792 | bytes 5423104 | tf_op jit(solution)/shard_map/bhd,bhde->bhe/dot_general | solution.py:155
  206.6 4.0 %all-to-all-start.5 = ((f32[4,2,4]{2,1,0:T(2,128)}), f32[4,2,4]{2,1,0:T(2,128)S(1)}, u32[]{:S(2)}, u32[]{:S(2)}) async-start(f32[4,2,4]{2,1,0:T(2,128)} %broadcast_in_dim.28), calls=%async_computation.5 | async-start | bytes 8192 | tf_op jit(solution)/shard_map/all_to_all | solution.py:42
  210.6 4.1 %all-to-all-done.5 = f32[4,2,4]{2,1,0:T(2,128)S(1)} async-done(((f32[4,2,4]{2,1,0:T(2,128)}), f32[4,2,4]{2,1,0:T(2,128)S(1)}, u32[]{:S(2)}, u32[]{:S(2)}) %all-to-all-start.5) | async-done | bytes 160 | tf_op jit(solution)/shard_map/all_to_all | solution.py:42
  214.8 9.5 %multiply_reduce_fusion = (f32[512]{0:T(512)S(1)}, f32[512,16,128]{0,2,1:T(8,128)}) fusion(f32[16,128,128]{2,1,0:T(8,128)S(1)} %copy-done.3, f32[32,128,128]{2,1,0:T(8,128)} %all-gather.8.cloned.1.call-done, f32[1,16,128,128]{3,2,1,0:T(8,128)} %get-tuple-element.2, f32[16,128,128]{2,1,0:T(8,128)} %get-tuple-element.3, ...), kind=kOutput, calls=%fused_computation.7 | convolution fusion | flops 278134272 | bytes 25167886 | tf_op jit(solution)/shard_map/chd,hde->che/dot_general | solution.py:124
  224.9 3.2 %all-to-all-start = ((f32[4,1,512]{2,1,0:T(1,128)}), f32[4,1,512]{2,1,0:T(1,128)S(1)}, u32[]{:S(2)}, u32[]{:S(2)}) async-start(f32[4,1,512]{2,1,0:T(1,128)} %broadcast_in_dim.25), calls=%async_computation | async-start | bytes 16384 | tf_op jit(solution)/shard_map/all_to_all | solution.py:42
  228.9 5.4 %copy.61 = f32[512,2048]{1,0:T(8,128)} copy(f32[512,2048]{0,1:T(8,128)} %bitcast.138) | data formatting | bytes 8388608 | tf_op jit(solution)/shard_map/reshape | solution.py:130
  234.3 3.9 %multiply_convert_fusion = bf16[512,2048]{1,0:T(8,128)(2,1)} fusion(f32[512,2048]{1,0:T(8,128)} %copy.61, f32[2048]{0:T(1024)S(1)} %copy-done.5, f32[512]{0:T(512)S(1)} %add_rsqrt_fusion), kind=kLoop, calls=%fused_computation.6 | loop fusion | flops 3145728 | bytes 6301696 | tf_op jit(solution)/shard_map/convert_element_type | solution.py:134
  (55 shorter events, 4.7 us)
Async XLA Ops:
  7.2 168.0 %copy-start = (bf16[512,2048]{1,0:T(8,128)(2,1)S(1)}, bf16[512,2048]{1,0:T(8,128)(2,1)}, u32[]{:S(2)}) copy-start(bf16[512,2048]{1,0:T(8,128)(2,1)} %param.10) | copy-start | bytes 6291460
  7.2 28.7 %all-gather.8.cloned.1.call-start = ((), (), s32[]{:S(2)}) async-start(), calls=%async_computation.7 | async-start | bytes 3145728 | tf_op jit(solution)/shard_map/all_gather | solution.py:23
  15.3 118.0 %all-gather.10.cloned.1.call-start = ((), (), s32[]{:S(2)}) async-start(), calls=%async_computation.8 | async-start | bytes 9437184 | tf_op jit(solution)/shard_map/all_gather | solution.py:23
  38.6 100.4 %copy-start.2 = (f32[16,128,128]{2,1,0:T(8,128)S(1)}, f32[16,128,128]{2,1,0:T(8,128)}, u32[]{:S(2)}) copy-start(f32[16,128,128]{2,1,0:T(8,128)} %fusion.9) | copy-start | bytes 3145732
  38.6 176.1 %all-gather.6.cloned.1.call-start = ((), (), s32[]{:S(2)}) async-start(), calls=%async_computation.6 | async-start | bytes 5242880 | tf_op jit(solution)/shard_map/all_gather | solution.py:23
  139.1 12.9 %copy-start.9 = (s32[4]{0:T(128)S(1)}, s32[4]{0:T(128)}, u32[]{:S(2)}) copy-start(s32[4]{0:T(128)} %param.15) | copy-start | bytes 52
  139.1 12.9 %copy-start.8 = (bf16[2,4,2048]{2,1,0:T(4,128)(2,1)S(1)}, bf16[2,4,2048]{2,1,0:T(4,128)(2,1)}, u32[]{:S(2)}) copy-start(bf16[2,4,2048]{2,1,0:T(4,128)(2,1)} %param.16) | copy-start | bytes 98308
  145.1 21.1 %all-to-all-start.2 = ((f32[32,32,128]{2,1,0:T(8,128)}), f32[32,32,128]{2,1,0:T(8,128)S(1)}, u32[]{:S(2)}, u32[]{:S(2)}) async-start(f32[32,32,128]{2,1,0:T(8,128)} %reduce_sum.56), calls=%async_computation.2 | async-start | bytes 1048576 | tf_op jit(solution)/shard_map/all_to_all | solution.py:75
  152.1 3.3 %copy-start.6 = (bf16[2,4,2048]{2,1,0:T(4,128)(2,1)S(1)}, bf16[2,4,2048]{2,1,0:T(4,128)(2,1)}, u32[]{:S(2)}) copy-start(bf16[2,4,2048]{2,1,0:T(4,128)(2,1)} %param.17) | copy-start | bytes 98308
  155.5 4.0 %copy-start.7 = (bf16[2,4,2048]{2,1,0:T(4,128)(2,1)S(1)}, bf16[2,4,2048]{2,1,0:T(4,128)(2,1)}, u32[]{:S(2)}) copy-start(bf16[2,4,2048]{2,1,0:T(4,128)(2,1)} %param.18) | copy-start | bytes 98308
  167.1 22.3 %all-to-all-start.3 = ((f32[32,32,128]{2,1,0:T(8,128)}), f32[32,32,128]{2,1,0:T(8,128)S(1)}, u32[]{:S(2)}, u32[]{:S(2)}) async-start(f32[32,32,128]{2,1,0:T(8,128)} %broadcast_in_dim.26), calls=%async_computation.3 | async-start | bytes 1048576 | tf_op jit(solution)/shard_map/all_to_all | solution.py:42
  189.5 8.2 %copy-start.1 = (f32[4,16,128,128]{3,2,1,0:T(8,128)S(1)}, f32[4,16,128,128]{3,2,1,0:T(8,128)}, u32[]{:S(2)}) copy-start(f32[4,16,128,128]{3,2,1,0:T(8,128)} %fusion.5) | copy-start | bytes 12582916
  197.7 2.7 %copy-start.4 = (f32[2,32,32,128]{3,2,0,1:T(8,128)}, f32[2,32,32,128]{3,2,0,1:T(8,128)S(1)}, u32[]{:S(2)}) copy-start(f32[2,32,32,128]{3,2,0,1:T(8,128)S(1)} %copy.63) | copy-start | bytes 3145732
  200.5 14.3 %copy-start.3 = (f32[16,128,128]{2,1,0:T(8,128)S(1)}, f32[16,128,128]{2,1,0:T(8,128)}, u32[]{:S(2)}) copy-start(f32[16,128,128]{2,1,0:T(8,128)} %slice_add_fusion.8) | copy-start | bytes 3145732
  206.6 8.1 %all-to-all-start.5 = ((f32[4,2,4]{2,1,0:T(2,128)}), f32[4,2,4]{2,1,0:T(2,128)S(1)}, u32[]{:S(2)}, u32[]{:S(2)}) async-start(f32[4,2,4]{2,1,0:T(2,128)} %broadcast_in_dim.28), calls=%async_computation.5 | async-start | bytes 8192 | tf_op jit(solution)/shard_map/all_to_all | solution.py:42
  214.8 13.4 %copy-start.5 = (f32[2048]{0:T(1024)S(1)}, f32[2048]{0:T(1024)}, u32[]{:S(2)}) copy-start(f32[2048]{0:T(1024)} %param.19) | copy-start | bytes 24580
  224.9 9.4 %all-to-all-start = ((f32[4,1,512]{2,1,0:T(1,128)}), f32[4,1,512]{2,1,0:T(1,128)S(1)}, u32[]{:S(2)}, u32[]{:S(2)}) async-start(f32[4,1,512]{2,1,0:T(1,128)} %broadcast_in_dim.25), calls=%async_computation | async-start | bytes 16384 | tf_op jit(solution)/shard_map/all_to_all | solution.py:42
Sparse Core Ops, SparseCore 0:
  15.4 20.4 all-gather.7
  38.8 94.4 all-gather.9
  139.1 60.6 all-gather.5
where the time goes:
time: 247 us; the launch traced here: 245 us
  waiting for transfers between devices  126 us (51%)
  matrix products  35.7 us (14%)
  starting transfers between devices  22.3 us (9%)
  other arithmetic  17.7 us (7%)
  local copies, waits for them, and re-layouts  16 us (6%)
  between operations  14 us (6%)
  blocking collectives  13.2 us (5%)
    all_gather x3, waiting for transfers between devices, entering(): pieces = lax.all_gather(subtotal, axis)  115 us
    all_to_all x3, starting transfers between devices, copy_for_each(): lax.all_to_all(jnp.broadcast_to(array[None], (peers, *array.shape)), axis...  15.3 us
    dot_general x1, matrix products, on_device(): jnp.einsum('chd,hde->che', block_queries, prior.astype(jnp.bfloat16), pre...  9.5 us
    dot_general x1, matrix products, on_device(): jnp.einsum('hcs,she->che', scores, block_values, preferred_element_type=j...  9.28 us
    all_to_all x3, waiting for transfers between devices, copy_for_each(): lax.all_to_all(jnp.broadcast_to(array[None], (peers, *array.shape)), axis...  9.04 us
    add x2, other arithmetic, add_states(): return earlier + later  8.44 us
    all_to_all x1, blocking collectives, copy_for_each(): lax.all_to_all(jnp.broadcast_to(array[None], (peers, *array.shape)), axis...  8.13 us
    dot_general x2, matrix products, on_device(): raw = jnp.einsum('bhd,bhde->bhe', new_query, state, precision=HIGHEST_PREC)  8.09 us
  transfers between devices with their start and end apart: 7, of which 5 were waited for; matrix products, arithmetic and copies ran while one was open for 16% of the time, Pallas kernels for 0%

commit v1 on v0

v1 whole, which is shorter than its diff:
```python
import jax
import jax.numpy as jnp
from jax import lax
from jax.experimental import pallas as pl
from jax.experimental.pallas import tpu as pltpu
from jax.sharding import Mesh
from jax.sharding import PartitionSpec as P

D = 128
NY, NZ, NX = 4, 8, 4
AXES = {"sy": NY, "sz": NZ, "sc": 2, "head": NX}
SEQ = ("sy", "sz", "sc")
MESH = pl.DeviceIdType.MESH
F32 = jnp.float32
BF16 = jnp.bfloat16
FAR_FIRST = (4, 3, 5, 2, 6, 1, 7)
NEAR_FIRST = (1, 7, 2, 6, 3, 5, 4)


def dot(a, b, ca, cb):
    return lax.dot_general(a, b, (((ca,), (cb,)), ((), ())), preferred_element_type=F32)


def away(axis, step):
    size = AXES[axis]
    return {axis: lax.rem(lax.axis_index(axis) + step, size)}


def lanes(head):
    return pl.ds(pl.multiple_of(head * D, D), D)


def main_kernel(
    len_ref, q_hbm, k_hbm, v_hbm, sk_hbm, sv_hbm, tq_hbm, tk_hbm, tv_hbm,
    att_out, sums_out, raw_out,
    q, k, v, sk, sv, tq, tk, tv, q8, k8, v8, k8s, v8s, mask,
    att, attb, acc, own, xsend, xrecv, chip, recv1, rsend, yrecv, send3, recv3,
    fwd, frecv, msg, mrecv,
    ld, out_sem, x_s, x_r, a_s, a_r, y_s, y_r, b_s, b_r, f_s, f_r, g_s, g_r,
):
    y, z, c, x = (lax.axis_index(a) for a in ("sy", "sz", "sc", "head"))
    other = 1 - c
    partner = {"sc": other}
    barrier = pltpu.get_barrier_semaphore()
    peers = [partner]
    peers += [away("sz", d) for d in range(1, NZ)]
    peers += [away("sy", d) for d in range(1, NY)]
    peers += [away("head", d) for d in range(1, NX)]
    for peer in peers:
        pl.semaphore_signal(barrier, inc=1, device_id=peer, device_id_type=MESH)

    half = NZ * D
    theirs = pl.ds(pl.multiple_of(other * half, half), half)
    mine = pl.ds(pl.multiple_of(c * half, half), half)
    loads = []
    for src, dst in (
        (k_hbm.at[:, theirs], k.at[:, theirs]),
        (v_hbm.at[:, theirs], v.at[:, theirs]),
        (tq_hbm, tq),
        (k_hbm.at[:, mine], k.at[:, mine]),
        (v_hbm.at[:, mine], v.at[:, mine]),
        (q_hbm, q),
        (tk_hbm, tk),
        (tv_hbm, tv),
        (sk_hbm, sk),
        (sv_hbm, sv),
    ):
        copy = pltpu.make_async_copy(src, dst, ld.at[len(loads)])
        copy.start()
        loads.append(copy)

    def send(src, dst, s, r, peer):
        copy = pltpu.make_async_remote_copy(
            src_ref=src, dst_ref=dst, send_sem=s, recv_sem=r, device_id=peer, device_id_type=MESH
        )
        return copy

    loads[0].wait()
    loads[1].wait()
    loads[2].wait()
    q8[0:4, :] = tq[0].astype(F32)
    q8[4:8, :] = tq[1].astype(F32)

    def their_state(i, carry):
        cols = lanes(other * NZ + i)
        xsend[i, 0:D, :] = dot(k[:, cols], v[:, cols], 0, 0)
        xsend[i, D : D + 8, :] = q8[:, cols]
        return carry

    lax.fori_loop(0, NZ, their_state, 0)
    pl.semaphore_wait(barrier, len(peers))
    x_copies = []
    for i in range(NZ):
        copy = send(xsend.at[i], xrecv.at[i], x_s.at[i], x_r.at[i], partner)
        copy.start()
        x_copies.append(copy)

    loads[3].wait()
    loads[4].wait()

    def my_state(i, carry):
        cols = lanes(c * NZ + i)
        own[i] = dot(k[:, cols], v[:, cols], 0, 0)
        return carry

    lax.fori_loop(0, NZ, my_state, 0)
    for copy in x_copies:
        copy.wait_recv()

    def chip_sum(i, dst):
        dst[0:D, :] = own[i] + xrecv[i, 0:D, :]
        dst[D : D + 8, :] = q8[:, lanes(c * NZ + i)]
        dst[D + 8 : D + 16, :] = xrecv[i, D : D + 8, :]

    a_copies = {}
    for d in FAR_FIRST:
        i = lax.rem(z + d, NZ)
        chip_sum(i, chip.at[i])
        a_copies[d] = send(chip.at[i], recv1.at[z], a_s.at[d], a_r.at[d], away("sz", d))
        a_copies[d].start()
    chip_sum(z, recv1.at[z])

    loads[5].wait()
    rows = lax.broadcasted_iota(jnp.int32, (256, 256), 0)
    columns = lax.broadcasted_iota(jnp.int32, (256, 256), 1)
    causal = columns <= rows

    def intra(h, carry):
        cols = lanes(h)
        top, bottom = q[0:256, cols], q[256:512, cols]
        s00 = jnp.where(causal, dot(top, k[0:256, cols], 1, 1), 0.0).astype(BF16)
        att[0:256, cols] = dot(s00, v[0:256, cols], 1, 0)
        s10 = dot(bottom, k[0:256, cols], 1, 1).astype(BF16)
        s11 = jnp.where(causal, dot(bottom, k[256:512, cols], 1, 1), 0.0).astype(BF16)
        att[256:512, cols] = dot(s10, v[0:256, cols], 1, 0) + dot(s11, v[256:512, cols], 1, 0)
        return carry

    lax.fori_loop(0, 10, intra, 0)

    for d in FAR_FIRST:
        a_copies[d].wait_recv()
    total = recv1[0, 0:D, :]
    for j in range(1, NZ):
        total = total + recv1[j, 0:D, :]
    rsend[...] = total
    yrecv[y] = total
    y_copies = []
    for d in (2, 1, 3):
        copy = send(rsend, yrecv.at[y], y_s.at[d], y_r.at[d], away("sy", d))
        copy.start()
        y_copies.append(copy)

    for copy in loads[6:]:
        copy.wait()
    k8[0:4, :] = tk[0].astype(F32)
    k8[4:8, :] = tk[1].astype(F32)
    v8[0:4, :] = tv[0].astype(F32)
    v8[4:8, :] = tv[1].astype(F32)
    k8s[...] = jnp.zeros_like(k8s)
    v8s[...] = jnp.zeros_like(v8s)
    k8s[4:8, :] = tk[0].astype(F32)
    v8s[4:8, :] = tv[0].astype(F32)
    row = lax.rem(lax.broadcasted_iota(jnp.int32, (8, D), 0), 4)
    column = lax.broadcasted_iota(jnp.int32, (8, D), 1)
    for n in range(4):
        live = (row == n) & (column < len_ref[n])
        mask[:, n * D : (n + 1) * D] = jnp.where(live, 1.0, 0.0)

    def suffix(h, carry):
        cols = lanes(h)
        query = q8[:, cols]
        scores = dot(query.astype(BF16), sk[:, cols], 1, 1) * mask[...]
        high = scores.astype(BF16).astype(F32)
        both = jnp.concatenate([high, scores - high], axis=0).astype(BF16)
        parts = dot(both, sv[:, cols], 1, 0)
        raw = parts[0:8] + parts[8:16]
        raw = raw + jnp.sum(query * k8[:, cols], axis=1, keepdims=True) * v8[:, cols]
        raw = raw + jnp.sum(query * k8s[:, cols], axis=1, keepdims=True) * v8s[:, cols]
        raw_out[:, cols] = raw
        return carry

    lax.fori_loop(0, 16, suffix, 0)

    for copy in y_copies:
        copy.wait_recv()
    before = jnp.zeros((D, D), F32)
    total = jnp.zeros((D, D), F32)
    for j in range(NY):
        before = before + jnp.where(j < y, yrecv[j], 0.0)
        total = total + yrecv[j]
    high = total.astype(BF16)
    low = (total - high.astype(F32)).astype(BF16)
    asked = recv1[:, D : D + 16, :].reshape(NZ * 16, D).astype(BF16)
    told = dot(asked, high, 1, 0) + dot(asked, low, 1, 0)
    for j in range(NZ):
        send3[j, 0:D, :] = before
        send3[j, D : D + 16, :] = told[16 * j : 16 * (j + 1), :]
        before = before + recv1[j, 0:D, :]
    b_copies = {}
    for d in FAR_FIRST:
        b_copies[d] = send(
            send3.at[lax.rem(z + d, NZ)], recv3.at[z], b_s.at[d], b_r.at[d], away("sz", d)
        )
        b_copies[d].start()
    recv3[z] = send3[z]

    lax.fori_loop(10, 16, intra, 0)

    acc[...] = jnp.zeros_like(acc)

    def inter(h, prior):
        cols = lanes(h)
        low = prior.astype(BF16)
        for t in range(0, 512, 256):
            new = att[t : t + 256, cols] + dot(q[t : t + 256, cols], low, 1, 0)
            acc[t : t + 256, :] += new * new
            attb[t : t + 256, cols] = new.astype(BF16)

    f_copies = []
    for n, d in enumerate((0, *NEAR_FIRST)):
        if d:
            b_copies[d].wait_recv()
        i = lax.rem(z + NZ - d, NZ)
        state = recv3[i, 0:D, :]
        fwd[i, 0:D, :] = state + jnp.where(c == 0, own[i], 0.0)
        fwd[i, D : D + 16, :] = recv3[i, D : D + 16, :]
        copy = send(fwd.at[i], frecv.at[i], f_s.at[n], f_r.at[n], partner)
        copy.start()
        f_copies.append(copy)
        inter(c * NZ + i, state + jnp.where(c == 1, xrecv[i, 0:D, :], 0.0))
        cols = lanes(c * NZ + i)
        raw_out[:, cols] = raw_out[:, cols] + recv3[i, D : D + 8, :]
    outs = [pltpu.make_async_copy(attb.at[:, mine], att_out.at[:, mine], out_sem.at[0])]
    outs[0].start()
    for n, d in enumerate((0, *NEAR_FIRST)):
        f_copies[n].wait_recv()
        i = lax.rem(z + NZ - d, NZ)
        inter(other * NZ + i, frecv[i, 0:D, :])
        cols = lanes(other * NZ + i)
        raw_out[:, cols] = raw_out[:, cols] + frecv[i, D + 8 : D + 16, :]
    outs.append(pltpu.make_async_copy(attb.at[:, theirs], att_out.at[:, theirs], out_sem.at[1]))
    outs[1].start()

    msg[:, 0:512] = lax.dot_general(
        jnp.ones((8, D), F32),
        acc[...],
        (((1,), (1,)), ((), ())),
        precision=lax.Precision.HIGHEST,
        preferred_element_type=F32,
    )
    squares = jnp.zeros((8, D), F32)
    for h in range(16):
        piece = raw_out[:, h * D : (h + 1) * D]
        squares = squares + piece * piece
    msg[:, 512:640] = jnp.broadcast_to(jnp.sum(squares, axis=1, keepdims=True), (8, D))
    g_copies = []
    for d in (2, 1, 3):
        copy = send(msg, mrecv.at[x], g_s.at[d], g_r.at[d], away("head", d))
        copy.start()
        g_copies.append(copy)
    mrecv[x] = msg[...]
    for copy in g_copies:
        copy.wait_recv()
    sums_out[...] = (mrecv[0] + mrecv[1]) + (mrecv[2] + mrecv[3])
    for copy in outs:
        copy.wait()
    for copy in (*x_copies, *a_copies.values(), *y_copies, *b_copies.values(), *f_copies, *g_copies):
        copy.wait_send()


def scale_kernel(att, sums, last, raw, gain, out, dec):
    total = jnp.broadcast_to(sums[0:1, :], (D, D)).T
    scale = lax.rsqrt(total / 8192.0 + 1e-06)
    for h in range(16):
        cols = slice(h * D, (h + 1) * D)
        out[:, cols] = (att[:, cols].astype(F32) * scale * gain[:, cols]).astype(BF16)

    @pl.when(pl.program_id(0) == 0)
    def _():
        steps = lax.rsqrt(last[:, 0:1] / 8192.0 + 1e-06)
        value = (raw[...] * steps * gain[...]).astype(BF16)
        dec[0] = value[0:4]
        dec[1] = value[4:8]


def on_device(q, k, v, sk, sv, lengths, tq, tk, tv, gain):
    rows, width = q.shape
    sk = sk.reshape(-1, width)
    sv = sv.reshape(-1, width)
    anywhere = pl.BlockSpec(memory_space=pl.ANY)
    vmem = pl.BlockSpec(memory_space=pltpu.VMEM)
    dma = pltpu.SemaphoreType.DMA
    steps = tq.shape

    def f32(*shape):
        return pltpu.VMEM(shape, F32)

    def bf16(*shape):
        return pltpu.VMEM(shape, BF16)

    att, sums, raw = pl.pallas_call(
        main_kernel,
        out_shape=(
            jax.ShapeDtypeStruct((rows, width), BF16),
            jax.ShapeDtypeStruct((8, 640), F32),
            jax.ShapeDtypeStruct((8, width), F32),
        ),
        in_specs=[pl.BlockSpec(memory_space=pltpu.SMEM)] + [anywhere] * 8,
        out_specs=(anywhere, vmem, vmem),
        scratch_shapes=[
            *[bf16(rows, width) for _ in range(5)],
            *[bf16(*steps) for _ in range(3)],
            *[f32(8, width) for _ in range(5)],
            f32(8, 512),
            f32(rows, width),
            bf16(rows, width),
            f32(rows, D),
            f32(NZ, D, D),
            f32(NZ, D + 8, D),
            f32(NZ, D + 8, D),
            f32(NZ, D + 16, D),
            f32(NZ, D + 16, D),
            f32(D, D),
            f32(NY, D, D),
            f32(NZ, D + 16, D),
            f32(NZ, D + 16, D),
            f32(NZ, D + 16, D),
            f32(NZ, D + 16, D),
            f32(8, 640),
            f32(NX, 8, 640),
            dma((10,)),
            dma((2,)),
            *[dma((8,)) for _ in range(4)],
            *[dma((4,)) for _ in range(2)],
            *[dma((8,)) for _ in range(4)],
            *[dma((4,)) for _ in range(2)],
        ],
        compiler_params=pltpu.CompilerParams(
            collective_id=0, has_side_effects=True, vmem_limit_bytes=60 << 20
        ),
        name="main",
    )(lengths, q, k, v, sk, sv, tq, tk, tv)

    blocks = rows // D
    return pl.pallas_call(
        scale_kernel,
        grid=(blocks,),
        out_shape=(jax.ShapeDtypeStruct((rows, width), BF16), jax.ShapeDtypeStruct(steps, BF16)),
        in_specs=[
            pl.BlockSpec((D, width), lambda i: (i, 0)),
            pl.BlockSpec((8, D), lambda i: (0, i)),
            pl.BlockSpec((8, D), lambda i: (0, blocks)),
            pl.BlockSpec((8, width), lambda i: (0, 0)),
            pl.BlockSpec((1, width), lambda i: (0, 0)),
        ],
        out_specs=(
            pl.BlockSpec((D, width), lambda i: (i, 0)),
            pl.BlockSpec(steps, lambda i: (0, 0, 0)),
        ),
        compiler_params=pltpu.CompilerParams(dimension_semantics=("arbitrary",)),
        name="scale",
    )(att, sums, sums, raw, gain.reshape(1, width))


def solution(mesh):
    finer = Mesh(mesh.devices.reshape(NY, NZ, 2, NX), (*SEQ, "head"))
    return jax.shard_map(
        on_device,
        mesh=finer,
        in_specs=(
            P(SEQ, "head"),
            P(SEQ, "head"),
            P(SEQ, "head"),
            P(SEQ, None, "head"),
            P(SEQ, None, "head"),
            P(SEQ),
            P(None, SEQ, "head"),
            P(None, SEQ, "head"),
            P(None, SEQ, "head"),
            P("head"),
        ),
        out_specs=(P(SEQ, "head"), P(None, SEQ, "head")),
        check_vma=False,
    )
```

time: 247 us -> 61.3 us (0.25)
  waiting for transfers between devices: 126 us -> 0 us
  Pallas kernels: 0 us -> 60.5 us
  matrix products: 35.7 us -> 0 us
  starting transfers between devices: 22.3 us -> 0 us
  other arithmetic: 17.7 us -> 0 us
  local copies, waits for them, and re-layouts: 16 us -> 0 us
  between operations: 14 us -> 0.64 us
  blocking collectives: 13.2 us -> 0 us
    all_gather x3 -> x0, waiting for transfers between devices: 115 us -> none  [entering(): pieces = lax.all_gather(subtotal, axis)]
    pallas_call x0 -> x2, Pallas kernels: none -> 60.5 us  [the longest x1 56.2 us: on_device(): pl.pallas_call(main_kernel, out_shape=(jax.ShapeDtypeStruct((rows, width)...]
    dot_general x6 -> x0, matrix products: 35.7 us -> none  [the longest x1 9.5 us: on_device(): jnp.einsum('chd,hde->che', block_queries, prior.astype(jnp.bfloat16), pre...]
    all_to_all x4 -> x0, starting transfers between devices: 22.2 us -> none  [the longest x3 15.3 us: copy_for_each(): lax.all_to_all(jnp.broadcast_to(array[None], (peers, *array.shape)), axis...]
    reshape x3 -> x0, local copies, waits for them, and re-layouts: 13.4 us -> none  [the longest x1 5.4 us: on_device(): attended = (intra + inter).reshape(rows_here, heads_here * HEAD_DIM)]
    all_to_all x2 -> x0, blocking collectives: 13.2 us -> none  [the longest x1 8.13 us: copy_for_each(): lax.all_to_all(jnp.broadcast_to(array[None], (peers, *array.shape)), axis...]
    all_to_all x4 -> x0, waiting for transfers between devices: 10.7 us -> none  [the longest x3 9.04 us: copy_for_each(): lax.all_to_all(jnp.broadcast_to(array[None], (peers, *array.shape)), axis...]
    add x2 -> x0, other arithmetic: 8.44 us -> none  [add_states(): return earlier + later]
  transfers between devices with their start and end apart: 7 -> 0, of which waited for: 5 -> 0; matrix products, arithmetic and copies ran while one was open for 16% -> 0% of each run, Pallas kernels for 0% -> 0%
where the time goes in v1:
time: 61.3 us; the launch traced here: 61.1 us
  Pallas kernels  60.5 us (99%)
  between operations  0.64 us (1%)
    pallas_call x1, Pallas kernels, on_device(): pl.pallas_call(main_kernel, out_shape=(jax.ShapeDtypeStruct((rows, width)...  56.2 us
    pallas_call x1, Pallas kernels, on_device(): pl.pallas_call(scale_kernel, grid=(blocks,), out_shape=(jax.ShapeDtypeStr...  4.27 us

profile of v1, /device:TPU:1, one launch (start us, length us, event | category | flops | bytes accessed | tf_op | source)
XLA Modules:
  0.0 61.1 jit_solution(1047596121782760369)
XLA Ops:
  0.6 56.2 %main.1 = (bf16[512,2048]{1,0:T(8,128)(2,1)}, f32[8,640]{1,0:T(8,128)}, f32[8,2048]{1,0:T(8,128)}) custom-call(s32[4]{0:T(128)} %len_ref.1, bf16[512,2048]{1,0:T(8,128)(2,1)} %q_hbm.1, bf16[512,2048]{1,0:T(8,128)(2,1)} %k_hbm.1, bf16[512,2048]{1,0:T(8,128)(2,1)} %v_hbm.1, bf16[512,2048]{1,0:T(8,128)(2,1)} %bitcast.3, bf16[512,2048]{1,0:T(8,128)(2,1)} %bitcast.4, ...), custom_call_target="tpu_custom_call" | custom-call | tf_op jit(solution)/shard_map/main/pallas_call | solution.py:301
  56.8 4.3 %scale.1 = (bf16[512,2048]{1,0:T(8,128)(2,1)}, bf16[2,4,2048]{2,1,0:T(4,128)(2,1)}) custom-call(bf16[512,2048]{1,0:T(8,128)(2,1)} %get-tuple-element.5.att, f32[8,640]{1,0:T(8,128)} %get-tuple-element.6.sums.last, f32[8,640]{1,0:T(8,128)} %get-tuple-element.6.sums.last, f32[8,2048]{1,0:T(8,128)} %get-tuple-element.7.raw, f32[1,2048]{1,0:T(1,128)} %bitcast.5), custom_call_target="tpu_custom_call" | custom-call | tf_op jit(solution)/shard_map/scale/pallas_call | solution.py:345

commit v2 on v1

--- a/solution.py
+++ b/solution.py
@@ -13,8 +13,9 @@
 MESH = pl.DeviceIdType.MESH
 F32 = jnp.float32
 BF16 = jnp.bfloat16
+CHUNKS = 4
+MAIN_VMEM = 36 << 20
 FAR_FIRST = (4, 3, 5, 2, 6, 1, 7)
-NEAR_FIRST = (1, 7, 2, 6, 3, 5, 4)
 
 
 def dot(a, b, ca, cb):
@@ -35,7 +36,7 @@
     att_out, sums_out, raw_out,
     q, k, v, sk, sv, tq, tk, tv, q8, k8, v8, k8s, v8s, mask,
     att, attb, acc, own, xsend, xrecv, chip, recv1, rsend, yrecv, send3, recv3,
-    fwd, frecv, msg, mrecv,
+    fwd, frecv, final, msg, mrecv,
     ld, out_sem, x_s, x_r, a_s, a_r, y_s, y_r, b_s, b_r, f_s, f_r, g_s, g_r,
 ):
     y, z, c, x = (lax.axis_index(a) for a in ("sy", "sz", "sc", "head"))
@@ -49,25 +50,23 @@
     for peer in peers:
         pl.semaphore_signal(barrier, inc=1, device_id=peer, device_id_type=MESH)
 
-    half = NZ * D
-    theirs = pl.ds(pl.multiple_of(other * half, half), half)
-    mine = pl.ds(pl.multiple_of(c * half, half), half)
+    quarter = NZ * D // 2
+
+    def part_of(core, n):
+        return pl.ds(pl.multiple_of((2 * core + n) * quarter, quarter), quarter)
+
     loads = []
-    for src, dst in (
-        (k_hbm.at[:, theirs], k.at[:, theirs]),
-        (v_hbm.at[:, theirs], v.at[:, theirs]),
-        (tq_hbm, tq),
-        (k_hbm.at[:, mine], k.at[:, mine]),
-        (v_hbm.at[:, mine], v.at[:, mine]),
-        (q_hbm, q),
-        (tk_hbm, tk),
-        (tv_hbm, tv),
-        (sk_hbm, sk),
-        (sv_hbm, sv),
-    ):
-        copy = pltpu.make_async_copy(src, dst, ld.at[len(loads)])
+    for core in (other, c):
+        for n in range(2):
+            cols = part_of(core, n)
+            loads.append((k_hbm.at[:, cols], k.at[:, cols]))
+            loads.append((v_hbm.at[:, cols], v.at[:, cols]))
+        if core is other:
+            loads.append((tq_hbm, tq))
+    loads += [(q_hbm, q), (tk_hbm, tk), (tv_hbm, tv), (sk_hbm, sk), (sv_hbm, sv)]
+    loads = [pltpu.make_async_copy(src, dst, ld.at[n]) for n, (src, dst) in enumerate(loads)]
+    for copy in loads:
         copy.start()
-        loads.append(copy)
 
     def send(src, dst, s, r, peer):
         copy = pltpu.make_async_remote_copy(
@@ -75,19 +74,20 @@
         )
         return copy
 
-    loads[0].wait()
-    loads[1].wait()
-    loads[2].wait()
-    q8[0:4, :] = tq[0].astype(F32)
-    q8[4:8, :] = tq[1].astype(F32)
-
     def their_state(i, carry):
         cols = lanes(other * NZ + i)
         xsend[i, 0:D, :] = dot(k[:, cols], v[:, cols], 0, 0)
-        xsend[i, D : D + 8, :] = q8[:, cols]
         return carry
 
-    lax.fori_loop(0, NZ, their_state, 0)
+    for n in range(2):
+        loads[2 * n].wait()
+        loads[2 * n + 1].wait()
+        lax.fori_loop(4 * n, 4 * n + 4, their_state, 0, unroll=4)
+    loads[4].wait()
+    q8[0:4, :] = tq[0].astype(F32)
+    q8[4:8, :] = tq[1].astype(F32)
+    for i in range(NZ):
+        xsend[i, D : D + 8, :] = q8[:, lanes(other * NZ + i)]
     pl.semaphore_wait(barrier, len(peers))
     x_copies = []
     for i in range(NZ):
@@ -95,15 +95,15 @@
         copy.start()
         x_copies.append(copy)
 
-    loads[3].wait()
-    loads[4].wait()
-
     def my_state(i, carry):
         cols = lanes(c * NZ + i)
         own[i] = dot(k[:, cols], v[:, cols], 0, 0)
         return carry
 
-    lax.fori_loop(0, NZ, my_state, 0)
+    for n in range(2):
+        loads[5 + 2 * n].wait()
+        loads[6 + 2 * n].wait()
+        lax.fori_loop(4 * n, 4 * n + 4, my_state, 0, unroll=4)
     for copy in x_copies:
         copy.wait_recv()
 
@@ -112,15 +112,27 @@
         dst[D : D + 8, :] = q8[:, lanes(c * NZ + i)]
         dst[D + 8 : D + 16, :] = xrecv[i, D : D + 8, :]
 
-    a_copies = {}
-    for d in FAR_FIRST:
+    def span(j):
+        first = j * D // CHUNKS
+        return pl.ds(first, (D + 16 if j == CHUNKS - 1 else first + D // CHUNKS) - first)
+
+    for d in range(1, NZ):
         i = lax.rem(z + d, NZ)
         chip_sum(i, chip.at[i])
-        a_copies[d] = send(chip.at[i], recv1.at[z], a_s.at[d], a_r.at[d], away("sz", d))
-        a_copies[d].start()
+    a_copies = {}
+    for j in range(CHUNKS):
+        for d in FAR_FIRST:
+            i = lax.rem(z + d, NZ)
+            a_copies[j, d] = send(
+                chip.at[i, span(j)],
+                recv1.at[z, span(j)],
+                a_s.at[j, d],
+                a_r.at[j, d],
+                away("sz", d),
+            )
+            a_copies[j, d].start()
     chip_sum(z, recv1.at[z])
 
-    loads[5].wait()
     rows = lax.broadcasted_iota(jnp.int32, (256, 256), 0)
     columns = lax.broadcasted_iota(jnp.int32, (256, 256), 1)
     causal = columns <= rows
@@ -135,36 +147,38 @@
         att[256:512, cols] = dot(s10, v[0:256, cols], 1, 0) + dot(s11, v[256:512, cols], 1, 0)
         return carry
 
-    lax.fori_loop(0, 10, intra, 0)
-
-    for d in FAR_FIRST:
-        a_copies[d].wait_recv()
-    total = recv1[0, 0:D, :]
-    for j in range(1, NZ):
-        total = total + recv1[j, 0:D, :]
-    rsend[...] = total
-    yrecv[y] = total
-    y_copies = []
-    for d in (2, 1, 3):
-        copy = send(rsend, yrecv.at[y], y_s.at[d], y_r.at[d], away("sy", d))
-        copy.start()
-        y_copies.append(copy)
-
-    for copy in loads[6:]:
-        copy.wait()
-    k8[0:4, :] = tk[0].astype(F32)
-    k8[4:8, :] = tk[1].astype(F32)
-    v8[0:4, :] = tv[0].astype(F32)
-    v8[4:8, :] = tv[1].astype(F32)
-    k8s[...] = jnp.zeros_like(k8s)
-    v8s[...] = jnp.zeros_like(v8s)
-    k8s[4:8, :] = tk[0].astype(F32)
-    v8s[4:8, :] = tv[0].astype(F32)
-    row = lax.rem(lax.broadcasted_iota(jnp.int32, (8, D), 0), 4)
-    column = lax.broadcasted_iota(jnp.int32, (8, D), 1)
-    for n in range(4):
-        live = (row == n) & (column < len_ref[n])
-        mask[:, n * D : (n + 1) * D] = jnp.where(live, 1.0, 0.0)
+    def row_sum(j):
+        part = slice(j * D // CHUNKS, (j + 1) * D // CHUNKS)
+        for d in FAR_FIRST:
+            a_copies[j, d].wait_recv()
+        total = recv1[0, part, :]
+        for n in range(1, NZ):
+            total = total + recv1[n, part, :]
+        rsend[part, :] = total
+        yrecv[y, part, :] = total
+        for d in (2, 1, 3):
+            copy = send(
+                rsend.at[part], yrecv.at[y, part], y_s.at[j, d], y_r.at[j, d], away("sy", d)
+            )
+            copy.start()
+            y_copies[j, d] = copy
+
+    def ready_steps():
+        for copy in loads[10:]:
+            copy.wait()
+        k8[0:4, :] = tk[0].astype(F32)
+        k8[4:8, :] = tk[1].astype(F32)
+        v8[0:4, :] = tv[0].astype(F32)
+        v8[4:8, :] = tv[1].astype(F32)
+        k8s[...] = jnp.zeros_like(k8s)
+        v8s[...] = jnp.zeros_like(v8s)
+        k8s[4:8, :] = tk[0].astype(F32)
+        v8s[4:8, :] = tv[0].astype(F32)
+        row = lax.rem(lax.broadcasted_iota(jnp.int32, (8, D), 0), 4)
+        column = lax.broadcasted_iota(jnp.int32, (8, D), 1)
+        for n in range(4):
+            live = (row == n) & (column < len_ref[n])
+            mask[:, n * D : (n + 1) * D] = jnp.where(live, 1.0, 0.0)
 
     def suffix(h, carry):
         cols = lanes(h)
@@ -179,32 +193,53 @@
         raw_out[:, cols] = raw
         return carry
 
-    lax.fori_loop(0, 16, suffix, 0)
-
-    for copy in y_copies:
-        copy.wait_recv()
-    before = jnp.zeros((D, D), F32)
-    total = jnp.zeros((D, D), F32)
-    for j in range(NY):
-        before = before + jnp.where(j < y, yrecv[j], 0.0)
-        total = total + yrecv[j]
-    high = total.astype(BF16)
-    low = (total - high.astype(F32)).astype(BF16)
-    asked = recv1[:, D : D + 16, :].reshape(NZ * 16, D).astype(BF16)
-    told = dot(asked, high, 1, 0) + dot(asked, low, 1, 0)
-    for j in range(NZ):
-        send3[j, 0:D, :] = before
-        send3[j, D : D + 16, :] = told[16 * j : 16 * (j + 1), :]
-        before = before + recv1[j, 0:D, :]
-    b_copies = {}
-    for d in FAR_FIRST:
-        b_copies[d] = send(
-            send3.at[lax.rem(z + d, NZ)], recv3.at[z], b_s.at[d], b_r.at[d], away("sz", d)
-        )
-        b_copies[d].start()
+    def priors(j):
+        part = slice(j * D // CHUNKS, (j + 1) * D // CHUNKS)
+        for d in (2, 1, 3):
+            y_copies[j, d].wait_recv()
+        before = jnp.zeros((D // CHUNKS, D), F32)
+        total = jnp.zeros((D // CHUNKS, D), F32)
+        for n in range(NY):
+            before = before + jnp.where(n < y, yrecv[n, part, :], 0.0)
+            total = total + yrecv[n, part, :]
+        final[part, :] = total
+        for n in range(NZ):
+            send3[n, part, :] = before
+            before = before + recv1[n, part, :]
+        if j == CHUNKS - 1:
+            high = final[...].astype(BF16)
+            low = (final[...] - high.astype(F32)).astype(BF16)
+            asked = recv1[:, D : D + 16, :].reshape(NZ * 16, D).astype(BF16)
+            told = dot(asked, high, 1, 0) + dot(asked, low, 1, 0)
+            for n in range(NZ):
+                send3[n, D : D + 16, :] = told[16 * n : 16 * (n + 1), :]
+        for d in FAR_FIRST:
+            b_copies[j, d] = send(
+                send3.at[lax.rem(z + d, NZ), span(j)],
+                recv3.at[z, span(j)],
+                b_s.at[j, d],
+                b_r.at[j, d],
+                away("sz", d),
+            )
+            b_copies[j, d].start()
+
+    y_copies, b_copies = {}, {}
+    loads[9].wait()
+    lax.fori_loop(0, 12, intra, 0, unroll=2)
+    row_sum(0)
+    lax.fori_loop(12, 16, intra, 0, unroll=2)
+    row_sum(1)
+    ready_steps()
+    lax.fori_loop(0, 4, suffix, 0, unroll=2)
+    priors(0)
+    row_sum(2)
+    lax.fori_loop(4, 10, suffix, 0, unroll=2)
+    priors(1)
+    row_sum(3)
+    lax.fori_loop(10, 16, suffix, 0, unroll=2)
+    priors(2)
+    priors(3)
     recv3[z] = send3[z]
-
-    lax.fori_loop(10, 16, intra, 0)
 
     acc[...] = jnp.zeros_like(acc)
 
@@ -217,9 +252,13 @@
             attb[t : t + 256, cols] = new.astype(BF16)
 
     f_copies = []
-    for n, d in enumerate((0, *NEAR_FIRST)):
+    order = (0, *FAR_FIRST)
+
+    def direct(n):
+        d = order[n]
         if d:
-            b_copies[d].wait_recv()
+            for j in range(CHUNKS):
+                b_copies[j, d].wait_recv()
         i = lax.rem(z + NZ - d, NZ)
         state = recv3[i, 0:D, :]
         fwd[i, 0:D, :] = state + jnp.where(c == 0, own[i], 0.0)
@@ -230,16 +269,22 @@
         inter(c * NZ + i, state + jnp.where(c == 1, xrecv[i, 0:D, :], 0.0))
         cols = lanes(c * NZ + i)
         raw_out[:, cols] = raw_out[:, cols] + recv3[i, D : D + 8, :]
-    outs = [pltpu.make_async_copy(attb.at[:, mine], att_out.at[:, mine], out_sem.at[0])]
-    outs[0].start()
-    for n, d in enumerate((0, *NEAR_FIRST)):
+
+    def forwarded(n):
         f_copies[n].wait_recv()
-        i = lax.rem(z + NZ - d, NZ)
+        i = lax.rem(z + NZ - order[n], NZ)
         inter(other * NZ + i, frecv[i, 0:D, :])
         cols = lanes(other * NZ + i)
         raw_out[:, cols] = raw_out[:, cols] + frecv[i, D + 8 : D + 16, :]
-    outs.append(pltpu.make_async_copy(attb.at[:, theirs], att_out.at[:, theirs], out_sem.at[1]))
-    outs[1].start()
+
+    for n in range(NZ):
+        direct(n)
+        if n > 1:
+            forwarded(n - 2)
+    for n in range(NZ - 2, NZ):
+        forwarded(n)
+    outs = [pltpu.make_async_copy(attb, att_out, out_sem.at[0])]
+    outs[0].start()
 
     msg[:, 0:512] = lax.dot_general(
         jnp.ones((8, D), F32),
@@ -264,7 +309,7 @@
     sums_out[...] = (mrecv[0] + mrecv[1]) + (mrecv[2] + mrecv[3])
     for copy in outs:
         copy.wait()
-    for copy in (*x_copies, *a_copies.values(), *y_copies, *b_copies.values(), *f_copies, *g_copies):
+    for copy in (*x_copies, *a_copies.values(), *y_copies.values(), *b_copies.values(), *f_copies, *g_copies):
         copy.wait_send()
 
 
@@ -326,20 +371,23 @@
             f32(NZ, D + 16, D),
             f32(NZ, D + 16, D),
             f32(NZ, D + 16, D),
+            f32(D, D),
             f32(8, 640),
             f32(NX, 8, 640),
-            dma((10,)),
-            dma((2,)),
-            *[dma((8,)) for _ in range(4)],
-            *[dma((4,)) for _ in range(2)],
-            *[dma((8,)) for _ in range(4)],
+            dma((14,)),
+            dma((1,)),
+            *[dma((8,)) for _ in range(2)],
+            *[dma((CHUNKS, 8)) for _ in range(2)],
+            *[dma((CHUNKS, 4)) for _ in range(2)],
+            *[dma((CHUNKS, 8)) for _ in range(2)],
+            *[dma((8,)) for _ in range(2)],
             *[dma((4,)) for _ in range(2)],
         ],
         compiler_params=pltpu.CompilerParams(
-            collective_id=0, has_side_effects=True, vmem_limit_bytes=60 << 20
+            collective_id=0, has_side_effects=True, vmem_limit_bytes=MAIN_VMEM
         ),
         name="main",
-    )(lengths, q, k, v, sk, sv, tq, tk, tv)
+    )(*(pltpu.with_memory_space_constraint(a, pltpu.HBM) for a in (lengths, q, k, v, sk, sv, tq, tk, tv)))
 
     blocks = rows // D
     return pl.pallas_call(
@@ -357,7 +405,7 @@
             pl.BlockSpec((D, width), lambda i: (i, 0)),
             pl.BlockSpec(steps, lambda i: (0, 0, 0)),
         ),
-        compiler_params=pltpu.CompilerParams(dimension_semantics=("arbitrary",)),
+        compiler_params=pltpu.CompilerParams(dimension_semantics=("arbitrary",), vmem_limit_bytes=12 << 20),
         name="scale",
     )(att, sums, sums, raw, gain.reshape(1, width))
 

time: 61.3 us -> 51.4 us (0.84)
  Pallas kernels: 60.5 us -> 50.6 us
    pallas_call x1, Pallas kernels: 56.2 us -> 48.2 us  [on_device(): pl.pallas_call(main_kernel, out_shape=(jax.ShapeDtypeStruct((rows, width)...]
    pallas_call x1, Pallas kernels: 4.27 us -> 2.39 us  [on_device(): pl.pallas_call(scale_kernel, grid=(blocks,), out_shape=(jax.ShapeDtypeStr...]
where the time goes in v2:
time: 51.4 us; the launch traced here: 51.3 us
  Pallas kernels  50.6 us (98%)
  between operations  0.66 us (1%)
    pallas_call x1, Pallas kernels, on_device(): pl.pallas_call(main_kernel, out_shape=(jax.ShapeDtypeStruct((rows, width)...  48.2 us
    pallas_call x1, Pallas kernels, on_device(): pl.pallas_call(scale_kernel, grid=(blocks,), out_shape=(jax.ShapeDtypeStr...  2.39 us

profile of v2, /device:TPU:1, one launch (start us, length us, event | category | flops | bytes accessed | tf_op | source)
XLA Modules:
  0.0 51.3 jit_solution(3730535881431580402)
XLA Ops:
  0.6 0.0 copy-start
  0.6 48.2 %main.1 = (bf16[512,2048]{1,0:T(8,128)(2,1)S(1)}, f32[8,640]{1,0:T(8,128)S(1)}, f32[8,2048]{1,0:T(8,128)S(1)}) custom-call(s32[4]{0:T(128)} %len_ref.1, bf16[512,2048]{1,0:T(8,128)(2,1)} %q_hbm.1, bf16[512,2048]{1,0:T(8,128)(2,1)} %k_hbm.1, bf16[512,2048]{1,0:T(8,128)(2,1)} %v_hbm.1, bf16[512,2048]{1,0:T(8,128)(2,1)} %bitcast.4, bf16[512,2048]{1,0:T(8,128)(2,1)} %bitcast.5, ...), custom_call_target="tpu_custom_call" | custom-call | tf_op jit(solution)/shard_map/main/pallas_call | solution.py:346
  48.9 0.0 copy-done
  48.9 2.4 %scale.1 = (bf16[512,2048]{1,0:T(8,128)(2,1)}, bf16[2,4,2048]{2,1,0:T(4,128)(2,1)}) custom-call(bf16[512,2048]{1,0:T(8,128)(2,1)S(1)} %get-tuple-element.5.att, f32[8,640]{1,0:T(8,128)S(1)} %get-tuple-element.6.sums.last, f32[8,640]{1,0:T(8,128)S(1)} %get-tuple-element.6.sums.last, f32[8,2048]{1,0:T(8,128)S(1)} %get-tuple-element.7.raw, f32[1,2048]{1,0:T(1,128)S(1)} %bitcast.3), custom_call_target="tpu_custom_call" | custom-call | tf_op jit(solution)/shard_map/scale/pallas_call | solution.py:393
Async XLA Ops:
  0.6 48.2 %copy-start = (f32[2048]{0:T(1024)S(1)}, f32[2048]{0:T(1024)}, u32[]{:S(2)}) copy-start(f32[2048]{0:T(1024)} %param.19) | copy-start | bytes 24580

commit v3 on v2

v3 whole, which is shorter than its diff:
```python
import jax
import jax.numpy as jnp
from jax import lax
from jax.experimental import pallas as pl
from jax.experimental.pallas import tpu as pltpu
from jax.sharding import Mesh
from jax.sharding import PartitionSpec as P

D = 128
NY, NZ, NX = 4, 8, 4
AXES = {"sy": NY, "sz": NZ, "sc": 2, "head": NX}
SEQ = ("sy", "sz", "sc")
MESH = pl.DeviceIdType.MESH
F32 = jnp.float32
BF16 = jnp.bfloat16
CHUNKS = 4
MAIN_VMEM = 36 << 20
FAR_FIRST = (4, 3, 5, 2, 6, 1, 7)
WAIT_ORDER = (1, 7, 2, 6, 3, 5, 4)
PLAN = (
    ("intra", 0, 12),
    ("sum", 0),
    ("intra", 12, 16),
    ("sum", 1),
    ("steps",),
    ("suffix", 0, 4),
    ("prior", 0),
    ("sum", 2),
    ("suffix", 4, 10),
    ("prior", 1),
    ("suffix", 10, 16),
    ("sum", 3),
    ("prior", 2),
    ("prior", 3),
    ("answers",),
)


def dot(a, b, ca, cb):
    return lax.dot_general(a, b, (((ca,), (cb,)), ((), ())), preferred_element_type=F32)


def away(axis, step):
    size = AXES[axis]
    return {axis: lax.rem(lax.axis_index(axis) + step, size)}


def lanes(head):
    return pl.ds(pl.multiple_of(head * D, D), D)


def main_kernel(
    len_hbm, q_hbm, k_hbm, v_hbm, sk_hbm, sv_hbm, tq_hbm, tk_hbm, tv_hbm,
    att_out, sums_out, raw_hbm,
    len_ref, raw_out,
    q, k, v, sk, sv, tq, tk, tv, q8, k8, v8, k8s, v8s, mask,
    att, attb, acc, own, xsend, xrecv, chip, recv1, rsend, yrecv, send3, recv3,
    qrecv, fwd, frecv, rest, frest, final, msg,
    ld, out_sem, x_s, x_r, q_s, q_r, a_s, a_r, y_s, y_r, b_s, b_r, f_s, f_r, g_s, g_r,
):
    y, z, c, x = (lax.axis_index(a) for a in ("sy", "sz", "sc", "head"))
    other = 1 - c
    partner = {"sc": other}
    barrier = pltpu.get_barrier_semaphore()
    peers = [partner]
    peers += [away("sz", d) for d in range(1, NZ)]
    peers += [away("sz", d) | partner for d in range(1, NZ)]
    peers += [away("sy", d) for d in range(1, NY)]
    peers += [away("head", d) for d in range(1, NX)]
    for peer in peers:
        pl.semaphore_signal(barrier, inc=1, device_id=peer, device_id_type=MESH)

    quarter = NZ * D // 2

    def part_of(core, n):
        return pl.ds(pl.multiple_of((2 * core + n) * quarter, quarter), quarter)

    loads = []
    for n in range(2):
        for core in (other, c):
            cols = part_of(core, n)
            loads.append((k_hbm.at[:, cols], k.at[:, cols]))
            loads.append((v_hbm.at[:, cols], v.at[:, cols]))
        if n == 0:
            loads.append((tq_hbm, tq))
    loads += [(q_hbm, q), (len_hbm, len_ref), (tk_hbm, tk), (tv_hbm, tv), (sk_hbm, sk), (sv_hbm, sv)]
    loads = [pltpu.make_async_copy(src, dst, ld.at[n]) for n, (src, dst) in enumerate(loads)]
    for copy in loads:
        copy.start()

    def send(src, dst, s, r, peer):
        copy = pltpu.make_async_remote_copy(
            src_ref=src, dst_ref=dst, send_sem=s, recv_sem=r, device_id=peer, device_id_type=MESH
        )
        return copy

    def wait_bytes(ref, sem):
        pltpu.make_async_copy(ref, ref, sem).wait()

    def their_state(i, carry):
        cols = lanes(other * NZ + i)
        xsend[i] = dot(k[:, cols], v[:, cols], 0, 0)
        return carry

    def my_state(i, carry):
        cols = lanes(c * NZ + i)
        own[i] = dot(k[:, cols], v[:, cols], 0, 0)
        return carry

    def exchange(n):
        for i in range(4 * n, 4 * n + 4):
            send(xsend.at[i], xrecv.at[i], x_s, x_r, partner).start()

    loads[0].wait()
    loads[1].wait()
    lax.fori_loop(0, 4, their_state, 0, unroll=4)
    loads[4].wait()
    q8[0:4, :] = tq[0].astype(F32)
    q8[4:8, :] = tq[1].astype(F32)
    pl.semaphore_wait(barrier, len(peers))
    exchange(0)
    for d in (4, 3, 5, 2, 6, 1, 7, 0):
        for e in range(2):
            if d or e:
                core = other if e else c
                i = lax.rem(z + d, NZ)
                asking = q8.at[:, lanes(core * NZ + i)]
                send(asking, qrecv.at[z, c], q_s, q_r, {"sz": i, "sc": core}).start()
    qrecv[z, c] = q8[:, lanes(c * NZ + z)]
    loads[2].wait()
    loads[3].wait()
    lax.fori_loop(0, 4, my_state, 0, unroll=4)
    loads[5].wait()
    loads[6].wait()
    lax.fori_loop(4, 8, their_state, 0, unroll=4)
    exchange(1)
    loads[7].wait()
    loads[8].wait()
    lax.fori_loop(4, 8, my_state, 0, unroll=4)
    wait_bytes(xrecv, x_r)

    def chip_sum(i, dst):
        dst[...] = own[i] + xrecv[i]

    def span(j):
        first = j * D // CHUNKS
        return pl.ds(first, 16 if j == CHUNKS else D // CHUNKS)

    for d in range(1, NZ):
        i = lax.rem(z + d, NZ)
        chip_sum(i, chip.at[i])
    for j in range(CHUNKS):
        for d in FAR_FIRST:
            i = lax.rem(z + d, NZ)
            send(chip.at[i, span(j)], recv1.at[z, span(j)], a_s, a_r.at[j], {"sz": i}).start()
    chip_sum(z, recv1.at[z])

    rows = lax.broadcasted_iota(jnp.int32, (256, 256), 0)
    columns = lax.broadcasted_iota(jnp.int32, (256, 256), 1)
    causal = columns <= rows

    def intra(h, carry):
        cols = lanes(h)
        top, bottom = q[0:256, cols], q[256:512, cols]
        s00 = jnp.where(causal, dot(top, k[0:256, cols], 1, 1), 0.0).astype(BF16)
        att[0:256, cols] = dot(s00, v[0:256, cols], 1, 0)
        s10 = dot(bottom, k[0:256, cols], 1, 1).astype(BF16)
        s11 = jnp.where(causal, dot(bottom, k[256:512, cols], 1, 1), 0.0).astype(BF16)
        att[256:512, cols] = dot(s10, v[0:256, cols], 1, 0) + dot(s11, v[256:512, cols], 1, 0)
        return carry

    def row_sum(j):
        part = slice(j * D // CHUNKS, (j + 1) * D // CHUNKS)
        wait_bytes(recv1.at[0 : NZ - 1, part], a_r.at[j])
        total = recv1[0, part, :]
        for n in range(1, NZ):
            total = total + recv1[n, part, :]
        rsend[part, :] = total
        yrecv[y, part, :] = total
        for d in (2, 1, 3):
            send(rsend.at[part], yrecv.at[y, part], y_s, y_r.at[j], away("sy", d)).start()

    def ready_steps():
        for copy in loads[10:]:
            copy.wait()
        k8[0:4, :] = tk[0].astype(F32)
        k8[4:8, :] = tk[1].astype(F32)
        v8[0:4, :] = tv[0].astype(F32)
        v8[4:8, :] = tv[1].astype(F32)
        k8s[...] = jnp.zeros_like(k8s)
        v8s[...] = jnp.zeros_like(v8s)
        k8s[4:8, :] = tk[0].astype(F32)
        v8s[4:8, :] = tv[0].astype(F32)
        row = lax.rem(lax.broadcasted_iota(jnp.int32, (8, D), 0), 4)
        column = lax.broadcasted_iota(jnp.int32, (8, D), 1)
        for n in range(4):
            live = (row == n) & (column < len_ref[n])
            mask[:, n * D : (n + 1) * D] = jnp.where(live, 1.0, 0.0)

    def suffix(h, carry):
        cols = lanes(h)
        query = q8[:, cols]
        scores = dot(query.astype(BF16), sk[:, cols], 1, 1) * mask[...]
        high = scores.astype(BF16).astype(F32)
        both = jnp.concatenate([high, scores - high], axis=0).astype(BF16)
        parts = dot(both, sv[:, cols], 1, 0)
        raw = parts[0:8] + parts[8:16]
        raw = raw + jnp.sum(query * k8[:, cols], axis=1, keepdims=True) * v8[:, cols]
        raw = raw + jnp.sum(query * k8s[:, cols], axis=1, keepdims=True) * v8s[:, cols]
        raw_out[:, cols] = raw
        return carry

    def priors(j):
        part = slice(j * D // CHUNKS, (j + 1) * D // CHUNKS)
        wait_bytes(yrecv.at[0 : NY - 1, part], y_r.at[j])
        before = jnp.zeros((D // CHUNKS, D), F32)
        total = jnp.zeros((D // CHUNKS, D), F32)
        for n in range(NY):
            before = before + jnp.where(n < y, yrecv[n, part, :], 0.0)
            total = total + yrecv[n, part, :]
        final[part, :] = total
        for n in range(NZ):
            send3[n, part, :] = before
            before = before + recv1[n, part, :]
        ship(j)
        recv3[z, part, :] = send3[z, part, :]

    def ship(j):
        for d in FAR_FIRST:
            i = lax.rem(z + d, NZ)
            sem = b_r.at[0 if j == CHUNKS else d]
            send(send3.at[i, span(j)], recv3.at[z, span(j)], b_s, sem, {"sz": i}).start()

    def answers():
        wait_bytes(q8.at[:, 0 : 15 * D], q_r)
        high = final[...].astype(BF16)
        low = (final[...] - high.astype(F32)).astype(BF16)
        asked = qrecv[...].reshape(NZ * 16, D).astype(BF16)
        told = dot(asked, high, 1, 0) + dot(asked, low, 1, 0)
        for n in range(NZ):
            send3[n, D : D + 16, :] = told[16 * n : 16 * (n + 1), :]
        ship(CHUNKS)
        recv3[z, D : D + 16, :] = send3[z, D : D + 16, :]

    loads[9].wait()
    work = {
        "intra": lambda a, b: lax.fori_loop(a, b, intra, 0, unroll=2),
        "suffix": lambda a, b: lax.fori_loop(a, b, suffix, 0, unroll=2),
        "steps": ready_steps,
        "sum": row_sum,
        "prior": priors,
        "answers": answers,
    }
    for name, *args in PLAN:
        work[name](*args)

    acc[...] = jnp.zeros_like(acc)

    def inter(h, prior):
        cols = lanes(h)
        low = prior.astype(BF16)
        for t in range(0, 512, 256):
            new = att[t : t + 256, cols] + dot(q[t : t + 256, cols], low, 1, 0)
            acc[t : t + 256, :] += new * new
            attb[t : t + 256, cols] = new.astype(BF16)

    for d in (0, *WAIT_ORDER):
        i = lax.rem(z + NZ - d, NZ)
        if d:
            wait_bytes(recv3.at[i, 0:D], b_r.at[d])
        fwd[i] = recv3[i, 0:D, :] + jnp.where(c == 0, own[i], 0.0)
        send(fwd.at[i], frecv.at[i], f_s.at[0], f_r.at[0], partner).start()

    def own_inter(i, carry):
        inter(c * NZ + i, recv3[i, 0:D, :] + jnp.where(c == 1, xrecv[i], 0.0))
        return carry

    def their_inter(i, carry):
        inter(other * NZ + i, frecv[i])
        return carry

    lax.fori_loop(0, NZ, own_inter, 0, unroll=4)
    wait_bytes(recv3.at[0 : NZ - 1, D : D + 16], b_r.at[0])
    for i in range(NZ):
        rest[i] = recv3[i, pl.ds(pl.multiple_of(D + 8 * other, 8), 8), :]
    send(rest, frest, f_s.at[1], f_r.at[1], partner).start()
    wait_bytes(frecv, f_r.at[0])
    lax.fori_loop(0, NZ, their_inter, 0, unroll=4)
    wait_bytes(frest, f_r.at[1])
    for i in range(NZ):
        cols = lanes(c * NZ + i)
        mine = recv3[i, pl.ds(pl.multiple_of(D + 8 * c, 8), 8), :]
        raw_out[:, cols] = raw_out[:, cols] + mine
        cols = lanes(other * NZ + i)
        raw_out[:, cols] = raw_out[:, cols] + frest[i]
    outs = [pltpu.make_async_copy(attb, att_out, out_sem.at[0])]
    outs[0].start()
    outs.append(pltpu.make_async_copy(raw_out, raw_hbm, out_sem.at[1]))
    outs[1].start()

    squares = lax.dot_general(
        jnp.ones((8, D), F32),
        acc[...],
        (((1,), (1,)), ((), ())),
        precision=lax.Precision.HIGHEST,
        preferred_element_type=F32,
    )
    for n in range(4):
        msg[n : n + 1, :] = squares[0:1, n * D : (n + 1) * D]
        msg[n + 4 : n + 5, :] = squares[0:1, n * D : (n + 1) * D]
    squares = jnp.zeros((8, D), F32)
    for h in range(16):
        piece = raw_out[:, h * D : (h + 1) * D]
        squares = squares + piece * piece
    msg[8:16, :] = jnp.broadcast_to(jnp.sum(squares, axis=1, keepdims=True), (8, D))
    for d in (2, 1, 3):
        send(msg, sums_out.at[x], g_s, g_r, away("head", d)).start()
    outs.append(pltpu.make_async_copy(msg, sums_out.at[x], out_sem.at[2]))
    outs[2].start()
    wait_bytes(xsend, x_s)
    wait_bytes(q8.at[:, 0 : 15 * D], q_s)
    wait_bytes(chip.at[0 : NZ - 1], a_s)
    wait_bytes(yrecv.at[0 : NY - 1], y_s)
    wait_bytes(send3.at[0 : NZ - 1], b_s)
    wait_bytes(fwd, f_s.at[0])
    wait_bytes(rest, f_s.at[1])
    wait_bytes(sums_out.at[0 : NX - 1], g_s)
    wait_bytes(sums_out.at[0 : NX - 1], g_r)
    for copy in outs:
        copy.wait()


def scale_kernel(att, sums, raw, gain, out, dec):
    row = pl.ds(pl.program_id(0), 1)
    total = (sums[0, row, :] + sums[1, row, :]) + (sums[2, row, :] + sums[3, row, :])
    total = jnp.broadcast_to(total, (D, D)).T
    scale = lax.rsqrt(total / 8192.0 + 1e-06)
    for h in range(16):
        cols = slice(h * D, (h + 1) * D)
        out[:, cols] = (att[:, cols].astype(F32) * scale * gain[:, cols]).astype(BF16)

    @pl.when(pl.program_id(0) == 0)
    def _():
        steps = (sums[0, 8:16, 0:1] + sums[1, 8:16, 0:1]) + (sums[2, 8:16, 0:1] + sums[3, 8:16, 0:1])
        steps = lax.rsqrt(steps / 8192.0 + 1e-06)
        value = (raw[...] * steps * gain[...]).astype(BF16)
        dec[0] = value[0:4]
        dec[1] = value[4:8]


def on_device(q, k, v, sk, sv, lengths, tq, tk, tv, gain):
    rows, width = q.shape
    sk = sk.reshape(-1, width)
    sv = sv.reshape(-1, width)
    anywhere = pl.BlockSpec(memory_space=pl.ANY)
    dma = pltpu.SemaphoreType.DMA
    steps = tq.shape

    def f32(*shape):
        return pltpu.VMEM(shape, F32)

    def bf16(*shape):
        return pltpu.VMEM(shape, BF16)

    att, sums, raw = pl.pallas_call(
        main_kernel,
        out_shape=(
            jax.ShapeDtypeStruct((rows, width), BF16),
            jax.ShapeDtypeStruct((NX, 16, D), F32),
            jax.ShapeDtypeStruct((8, width), F32),
        ),
        in_specs=[anywhere] * 9,
        out_specs=(anywhere, anywhere, anywhere),
        scratch_shapes=[
            pltpu.SMEM((4,), jnp.int32),
            f32(8, width),
            *[bf16(rows, width) for _ in range(5)],
            *[bf16(*steps) for _ in range(3)],
            *[f32(8, width) for _ in range(5)],
            f32(8, 512),
            f32(rows, width),
            bf16(rows, width),
            f32(rows, D),
            f32(NZ, D, D),
            f32(NZ, D, D),
            f32(NZ, D, D),
            f32(NZ, D, D),
            f32(NZ, D, D),
            f32(D, D),
            f32(NY, D, D),
            f32(NZ, D + 16, D),
            f32(NZ, D + 16, D),
            f32(NZ, 2, 8, D),
            f32(NZ, D, D),
            f32(NZ, D, D),
            f32(NZ, 8, D),
            f32(NZ, 8, D),
            f32(D, D),
            f32(16, D),
            dma((15,)),
            dma((3,)),
            *[dma(()) for _ in range(4)],
            dma(()),
            dma((CHUNKS,)),
            dma(()),
            dma((CHUNKS,)),
            dma(()),
            dma((NZ,)),
            dma((2,)),
            dma((2,)),
            dma(()),
            dma(()),
        ],
        compiler_params=pltpu.CompilerParams(
            collective_id=0, has_side_effects=True, vmem_limit_bytes=MAIN_VMEM
        ),
        name="main",
    )(*(pltpu.with_memory_space_constraint(a, pltpu.HBM) for a in (lengths, q, k, v, sk, sv, tq, tk, tv)))

    blocks = rows // D
    return pl.pallas_call(
        scale_kernel,
        grid=(blocks,),
        out_shape=(jax.ShapeDtypeStruct((rows, width), BF16), jax.ShapeDtypeStruct(steps, BF16)),
        in_specs=[
            pl.BlockSpec((D, width), lambda i: (i, 0)),
            pl.BlockSpec((NX, 16, D), lambda i: (0, 0, 0)),
            pl.BlockSpec((8, width), lambda i: (0, 0)),
            pl.BlockSpec((1, width), lambda i: (0, 0)),
        ],
        out_specs=(
            pl.BlockSpec((D, width), lambda i: (i, 0)),
            pl.BlockSpec(steps, lambda i: (0, 0, 0)),
        ),
        compiler_params=pltpu.CompilerParams(dimension_semantics=("arbitrary",), vmem_limit_bytes=12 << 20),
        name="scale",
    )(att, sums, raw, gain.reshape(1, width))


def solution(mesh):
    finer = Mesh(mesh.devices.reshape(NY, NZ, 2, NX), (*SEQ, "head"))
    return jax.shard_map(
        on_device,
        mesh=finer,
        in_specs=(
            P(SEQ, "head"),
            P(SEQ, "head"),
            P(SEQ, "head"),
            P(SEQ, None, "head"),
            P(SEQ, None, "head"),
            P(SEQ),
            P(None, SEQ, "head"),
            P(None, SEQ, "head"),
            P(None, SEQ, "head"),
            P("head"),
        ),
        out_specs=(P(SEQ, "head"), P(None, SEQ, "head")),
        check_vma=False,
    )
```

time: 51.4 us -> 47 us (0.914)
  Pallas kernels: 50.6 us -> 46.2 us
    pallas_call x1, Pallas kernels: 48.2 us -> 43.8 us  [on_device(): pl.pallas_call(main_kernel, out_shape=(jax.ShapeDtypeStruct((rows, width)...]
where the time goes in v3:
time: 47 us; the launch traced here: 46.9 us
  Pallas kernels  46.2 us (98%)
  between operations  0.66 us (1%)
    pallas_call x1, Pallas kernels, on_device(): pl.pallas_call(main_kernel, out_shape=(jax.ShapeDtypeStruct((rows, width)...  43.8 us
    pallas_call x1, Pallas kernels, on_device(): pl.pallas_call(scale_kernel, grid=(blocks,), out_shape=(jax.ShapeDtypeStr...  2.39 us

profile of v3, /device:TPU:1, one launch (start us, length us, event | category | flops | bytes accessed | tf_op | source)
XLA Modules:
  0.0 46.9 jit_solution(11478821287633382771)
XLA Ops:
  0.6 0.0 copy-start
  0.6 43.8 %main.1 = (bf16[512,2048]{1,0:T(8,128)(2,1)S(1)}, f32[4,16,128]{2,1,0:T(8,128)S(1)}, f32[8,2048]{1,0:T(8,128)S(1)}) custom-call(s32[4]{0:T(128)} %len_hbm.1, bf16[512,2048]{1,0:T(8,128)(2,1)} %q_hbm.1, bf16[512,2048]{1,0:T(8,128)(2,1)} %k_hbm.1, bf16[512,2048]{1,0:T(8,128)(2,1)} %v_hbm.1, bf16[512,2048]{1,0:T(8,128)(2,1)} %bitcast.4, ...), custom_call_target="tpu_custom_call" | custom-call | tf_op jit(solution)/shard_map/main/pallas_call | solution.py:365
  44.5 0.0 copy-done
  44.5 2.4 %scale.1 = (bf16[512,2048]{1,0:T(8,128)(2,1)}, bf16[2,4,2048]{2,1,0:T(4,128)(2,1)}) custom-call(bf16[512,2048]{1,0:T(8,128)(2,1)S(1)} %get-tuple-element.5.att, f32[4,16,128]{2,1,0:T(8,128)S(1)} %get-tuple-element.6.sums, f32[8,2048]{1,0:T(8,128)S(1)} %get-tuple-element.7.raw, f32[1,2048]{1,0:T(1,128)S(1)} %bitcast.3), custom_call_target="tpu_custom_call" | custom-call | tf_op jit(solution)/shard_map/scale/pallas_call | solution.py:421
Async XLA Ops:
  0.6 43.8 %copy-start = (f32[2048]{0:T(1024)S(1)}, f32[2048]{0:T(1024)}, u32[]{:S(2)}) copy-start(f32[2048]{0:T(1024)} %param.19) | copy-start | bytes 24580

commit v4 on v3

--- a/solution.py
+++ b/solution.py
@@ -13,7 +13,8 @@
 MESH = pl.DeviceIdType.MESH
 F32 = jnp.float32
 BF16 = jnp.bfloat16
-CHUNKS = 4
+BOUNDS = (0, 32, 64, 96, 128)
+CHUNKS = len(BOUNDS) - 1
 MAIN_VMEM = 36 << 20
 FAR_FIRST = (4, 3, 5, 2, 6, 1, 7)
 WAIT_ORDER = (1, 7, 2, 6, 3, 5, 4)
@@ -55,8 +56,8 @@
     len_ref, raw_out,
     q, k, v, sk, sv, tq, tk, tv, q8, k8, v8, k8s, v8s, mask,
     att, attb, acc, own, xsend, xrecv, chip, recv1, rsend, yrecv, send3, recv3,
-    qrecv, fwd, frecv, rest, frest, final, msg,
-    ld, out_sem, x_s, x_r, q_s, q_r, a_s, a_r, y_s, y_r, b_s, b_r, f_s, f_r, g_s, g_r,
+    qrecv, fwd, frecv, tell, heard, final, msg,
+    ld, out_sem, x_s, x_r, q_s, q_r, a_s, a_r, y_s, y_r, b_s, b_r, f_s, f_r, t_s, t_r, g_s, g_r,
 ):
     y, z, c, x = (lax.axis_index(a) for a in ("sy", "sz", "sc", "head"))
     other = 1 - c
@@ -76,12 +77,12 @@
         return pl.ds(pl.multiple_of((2 * core + n) * quarter, quarter), quarter)
 
     loads = []
-    for n in range(2):
-        for core in (other, c):
+    for core in (other, c):
+        for n in range(2):
             cols = part_of(core, n)
             loads.append((k_hbm.at[:, cols], k.at[:, cols]))
             loads.append((v_hbm.at[:, cols], v.at[:, cols]))
-        if n == 0:
+        if core is other:
             loads.append((tq_hbm, tq))
     loads += [(q_hbm, q), (len_hbm, len_ref), (tk_hbm, tk), (tv_hbm, tv), (sk_hbm, sk), (sv_hbm, sv)]
     loads = [pltpu.make_async_copy(src, dst, ld.at[n]) for n, (src, dst) in enumerate(loads)]
@@ -107,18 +108,19 @@
         own[i] = dot(k[:, cols], v[:, cols], 0, 0)
         return carry
 
-    def exchange(n):
-        for i in range(4 * n, 4 * n + 4):
-            send(xsend.at[i], xrecv.at[i], x_s, x_r, partner).start()
-
-    loads[0].wait()
-    loads[1].wait()
-    lax.fori_loop(0, 4, their_state, 0, unroll=4)
+    for n in range(2):
+        loads[2 * n].wait()
+        loads[2 * n + 1].wait()
+        lax.fori_loop(4 * n, 4 * n + 4, their_state, 0, unroll=4)
     loads[4].wait()
     q8[0:4, :] = tq[0].astype(F32)
     q8[4:8, :] = tq[1].astype(F32)
+    loads[5].wait()
+    loads[6].wait()
+    lax.fori_loop(0, 4, my_state, 0, unroll=4)
     pl.semaphore_wait(barrier, len(peers))
-    exchange(0)
+    for i in range(NZ):
+        send(xsend.at[i], xrecv.at[i], x_s, x_r, partner).start()
     for d in (4, 3, 5, 2, 6, 1, 7, 0):
         for e in range(2):
             if d or e:
@@ -127,13 +129,6 @@
                 asking = q8.at[:, lanes(core * NZ + i)]
                 send(asking, qrecv.at[z, c], q_s, q_r, {"sz": i, "sc": core}).start()
     qrecv[z, c] = q8[:, lanes(c * NZ + z)]
-    loads[2].wait()
-    loads[3].wait()
-    lax.fori_loop(0, 4, my_state, 0, unroll=4)
-    loads[5].wait()
-    loads[6].wait()
-    lax.fori_loop(4, 8, their_state, 0, unroll=4)
-    exchange(1)
     loads[7].wait()
     loads[8].wait()
     lax.fori_loop(4, 8, my_state, 0, unroll=4)
@@ -143,8 +138,7 @@
         dst[...] = own[i] + xrecv[i]
 
     def span(j):
-        first = j * D // CHUNKS
-        return pl.ds(first, 16 if j == CHUNKS else D // CHUNKS)
+        return pl.ds(BOUNDS[j], BOUNDS[j + 1] - BOUNDS[j])
 
     for d in range(1, NZ):
         i = lax.rem(z + d, NZ)
@@ -170,7 +164,7 @@
         return carry
 
     def row_sum(j):
-        part = slice(j * D // CHUNKS, (j + 1) * D // CHUNKS)
+        part = slice(BOUNDS[j], BOUNDS[j + 1])
         wait_bytes(recv1.at[0 : NZ - 1, part], a_r.at[j])
         total = recv1[0, part, :]
         for n in range(1, NZ):
@@ -211,10 +205,10 @@
         return carry
 
     def priors(j):
-        part = slice(j * D // CHUNKS, (j + 1) * D // CHUNKS)
+        part = slice(BOUNDS[j], BOUNDS[j + 1])
         wait_bytes(yrecv.at[0 : NY - 1, part], y_r.at[j])
-        before = jnp.zeros((D // CHUNKS, D), F32)
-        total = jnp.zeros((D // CHUNKS, D), F32)
+        before = jnp.zeros((BOUNDS[j + 1] - BOUNDS[j], D), F32)
+        total = before
         for n in range(NY):
             before = before + jnp.where(n < y, yrecv[n, part, :], 0.0)
             total = total + yrecv[n, part, :]
@@ -228,8 +222,7 @@
     def ship(j):
         for d in FAR_FIRST:
             i = lax.rem(z + d, NZ)
-            sem = b_r.at[0 if j == CHUNKS else d]
-            send(send3.at[i, span(j)], recv3.at[z, span(j)], b_s, sem, {"sz": i}).start()
+            send(send3.at[i, span(j)], recv3.at[z, span(j)], b_s, b_r.at[d], {"sz": i}).start()
 
     def answers():
         wait_bytes(q8.at[:, 0 : 15 * D], q_r)
@@ -237,10 +230,15 @@
         low = (final[...] - high.astype(F32)).astype(BF16)
         asked = qrecv[...].reshape(NZ * 16, D).astype(BF16)
         told = dot(asked, high, 1, 0) + dot(asked, low, 1, 0)
-        for n in range(NZ):
-            send3[n, D : D + 16, :] = told[16 * n : 16 * (n + 1), :]
-        ship(CHUNKS)
-        recv3[z, D : D + 16, :] = send3[z, D : D + 16, :]
+        tell[...] = told.reshape(NZ, 2, 8, D)
+        for d in (4, 3, 5, 2, 6, 1, 7, 0):
+            for e in range(2):
+                if d or e:
+                    core = other if e else c
+                    i = lax.rem(z + d, NZ)
+                    slot = heard.at[c * NZ + z]
+                    send(tell.at[i, core], slot, t_s, t_r, {"sz": i, "sc": core}).start()
+        heard[c * NZ + z] = tell[z, c]
 
     loads[9].wait()
     work = {
@@ -267,12 +265,12 @@
     for d in (0, *WAIT_ORDER):
         i = lax.rem(z + NZ - d, NZ)
         if d:
-            wait_bytes(recv3.at[i, 0:D], b_r.at[d])
-        fwd[i] = recv3[i, 0:D, :] + jnp.where(c == 0, own[i], 0.0)
-        send(fwd.at[i], frecv.at[i], f_s.at[0], f_r.at[0], partner).start()
+            wait_bytes(recv3.at[i], b_r.at[d])
+        fwd[i] = recv3[i] + jnp.where(c == 0, own[i], 0.0)
+        send(fwd.at[i], frecv.at[i], f_s, f_r, partner).start()
 
     def own_inter(i, carry):
-        inter(c * NZ + i, recv3[i, 0:D, :] + jnp.where(c == 1, xrecv[i], 0.0))
+        inter(c * NZ + i, recv3[i] + jnp.where(c == 1, xrecv[i], 0.0))
         return carry
 
     def their_inter(i, carry):
@@ -280,23 +278,20 @@
         return carry
 
     lax.fori_loop(0, NZ, own_inter, 0, unroll=4)
-    wait_bytes(recv3.at[0 : NZ - 1, D : D + 16], b_r.at[0])
-    for i in range(NZ):
-        rest[i] = recv3[i, pl.ds(pl.multiple_of(D + 8 * other, 8), 8), :]
-    send(rest, frest, f_s.at[1], f_r.at[1], partner).start()
-    wait_bytes(frecv, f_r.at[0])
+    wait_bytes(heard.at[0:15], t_r)
+    squares = jnp.zeros((8, D), F32)
+    for h in range(16):
+        cols = slice(h * D, (h + 1) * D)
+        piece = raw_out[:, cols] + heard[h]
+        raw_out[:, cols] = piece
+        squares = squares + piece * piece
+    msg[8:16, :] = jnp.broadcast_to(jnp.sum(squares, axis=1, keepdims=True), (8, D))
+    raw_copy = pltpu.make_async_copy(raw_out, raw_hbm, out_sem.at[1])
+    raw_copy.start()
+    wait_bytes(frecv, f_r)
     lax.fori_loop(0, NZ, their_inter, 0, unroll=4)
-    wait_bytes(frest, f_r.at[1])
-    for i in range(NZ):
-        cols = lanes(c * NZ + i)
-        mine = recv3[i, pl.ds(pl.multiple_of(D + 8 * c, 8), 8), :]
-        raw_out[:, cols] = raw_out[:, cols] + mine
-        cols = lanes(other * NZ + i)
-        raw_out[:, cols] = raw_out[:, cols] + frest[i]
     outs = [pltpu.make_async_copy(attb, att_out, out_sem.at[0])]
     outs[0].start()
-    outs.append(pltpu.make_async_copy(raw_out, raw_hbm, out_sem.at[1]))
-    outs[1].start()
 
     squares = lax.dot_general(
         jnp.ones((8, D), F32),
@@ -308,44 +303,49 @@
     for n in range(4):
         msg[n : n + 1, :] = squares[0:1, n * D : (n + 1) * D]
         msg[n + 4 : n + 5, :] = squares[0:1, n * D : (n + 1) * D]
-    squares = jnp.zeros((8, D), F32)
-    for h in range(16):
-        piece = raw_out[:, h * D : (h + 1) * D]
-        squares = squares + piece * piece
-    msg[8:16, :] = jnp.broadcast_to(jnp.sum(squares, axis=1, keepdims=True), (8, D))
     for d in (2, 1, 3):
         send(msg, sums_out.at[x], g_s, g_r, away("head", d)).start()
     outs.append(pltpu.make_async_copy(msg, sums_out.at[x], out_sem.at[2]))
-    outs[2].start()
+    outs[1].start()
+    outs.append(raw_copy)
     wait_bytes(xsend, x_s)
     wait_bytes(q8.at[:, 0 : 15 * D], q_s)
     wait_bytes(chip.at[0 : NZ - 1], a_s)
     wait_bytes(yrecv.at[0 : NY - 1], y_s)
     wait_bytes(send3.at[0 : NZ - 1], b_s)
-    wait_bytes(fwd, f_s.at[0])
-    wait_bytes(rest, f_s.at[1])
+    wait_bytes(fwd, f_s)
+    wait_bytes(heard.at[0:15], t_s)
     wait_bytes(sums_out.at[0 : NX - 1], g_s)
     wait_bytes(sums_out.at[0 : NX - 1], g_r)
     for copy in outs:
         copy.wait()
 
 
-def scale_kernel(att, sums, raw, gain, out, dec):
-    row = pl.ds(pl.program_id(0), 1)
-    total = (sums[0, row, :] + sums[1, row, :]) + (sums[2, row, :] + sums[3, row, :])
-    total = jnp.broadcast_to(total, (D, D)).T
-    scale = lax.rsqrt(total / 8192.0 + 1e-06)
-    for h in range(16):
-        cols = slice(h * D, (h + 1) * D)
-        out[:, cols] = (att[:, cols].astype(F32) * scale * gain[:, cols]).astype(BF16)
-
-    @pl.when(pl.program_id(0) == 0)
-    def _():
-        steps = (sums[0, 8:16, 0:1] + sums[1, 8:16, 0:1]) + (sums[2, 8:16, 0:1] + sums[3, 8:16, 0:1])
-        steps = lax.rsqrt(steps / 8192.0 + 1e-06)
-        value = (raw[...] * steps * gain[...]).astype(BF16)
-        dec[0] = value[0:4]
-        dec[1] = value[4:8]
+def scale_kernel(att, sums, raw, gain, out, dec_out, held, dec, sem):
+    copies = []
+    for n in range(4):
+        total = (sums[0, n : n + 1, :] + sums[1, n : n + 1, :]) + (
+            sums[2, n : n + 1, :] + sums[3, n : n + 1, :]
+        )
+        scale = lax.rsqrt(jnp.broadcast_to(total, (D, D)).T / 8192.0 + 1e-06)
+        for m in range(2):
+            rows = slice(n * D + 64 * m, n * D + 64 * m + 64)
+            part = scale[64 * m : 64 * m + 64]
+            for h in range(16):
+                cols = slice(h * D, (h + 1) * D)
+                held[rows, cols] = (att[rows, cols].astype(F32) * part * gain[:, cols]).astype(BF16)
+            copy = pltpu.make_async_copy(held.at[rows], out.at[rows], sem.at[2 * n + m])
+            copy.start()
+            copies.append(copy)
+    steps = (sums[0, 8:16, 0:1] + sums[1, 8:16, 0:1]) + (sums[2, 8:16, 0:1] + sums[3, 8:16, 0:1])
+    steps = lax.rsqrt(steps / 8192.0 + 1e-06)
+    value = (raw[...] * steps * gain[...]).astype(BF16)
+    dec[0] = value[0:4]
+    dec[1] = value[4:8]
+    copies.append(pltpu.make_async_copy(dec, dec_out, sem.at[8]))
+    copies[8].start()
+    for copy in copies:
+        copy.wait()
 
 
 def on_device(q, k, v, sk, sv, lengths, tq, tk, tv, gain):
@@ -388,13 +388,13 @@
             f32(NZ, D, D),
             f32(D, D),
             f32(NY, D, D),
-            f32(NZ, D + 16, D),
-            f32(NZ, D + 16, D),
+            f32(NZ, D, D),
+            f32(NZ, D, D),
             f32(NZ, 2, 8, D),
             f32(NZ, D, D),
             f32(NZ, D, D),
-            f32(NZ, 8, D),
-            f32(NZ, 8, D),
+            f32(NZ, 2, 8, D),
+            f32(2 * NZ, 8, D),
             f32(D, D),
             f32(16, D),
             dma((15,)),
@@ -406,10 +406,7 @@
             dma((CHUNKS,)),
             dma(()),
             dma((NZ,)),
-            dma((2,)),
-            dma((2,)),
-            dma(()),
-            dma(()),
+            *[dma(()) for _ in range(6)],
         ],
         compiler_params=pltpu.CompilerParams(
             collective_id=0, has_side_effects=True, vmem_limit_bytes=MAIN_VMEM
@@ -417,22 +414,14 @@
         name="main",
     )(*(pltpu.with_memory_space_constraint(a, pltpu.HBM) for a in (lengths, q, k, v, sk, sv, tq, tk, tv)))
 
-    blocks = rows // D
+    vmem = pl.BlockSpec(memory_space=pltpu.VMEM)
     return pl.pallas_call(
         scale_kernel,
-        grid=(blocks,),
         out_shape=(jax.ShapeDtypeStruct((rows, width), BF16), jax.ShapeDtypeStruct(steps, BF16)),
-        in_specs=[
-            pl.BlockSpec((D, width), lambda i: (i, 0)),
-            pl.BlockSpec((NX, 16, D), lambda i: (0, 0, 0)),
-            pl.BlockSpec((8, width), lambda i: (0, 0)),
-            pl.BlockSpec((1, width), lambda i: (0, 0)),
-        ],
-        out_specs=(
-            pl.BlockSpec((D, width), lambda i: (i, 0)),
-            pl.BlockSpec(steps, lambda i: (0, 0, 0)),
-        ),
-        compiler_params=pltpu.CompilerParams(dimension_semantics=("arbitrary",), vmem_limit_bytes=12 << 20),
+        in_specs=[vmem] * 4,
+        out_specs=(anywhere, anywhere),
+        scratch_shapes=[bf16(rows, width), bf16(*steps), dma((9,))],
+        compiler_params=pltpu.CompilerParams(vmem_limit_bytes=12 << 20),
         name="scale",
     )(att, sums, raw, gain.reshape(1, width))
 

time: 47 us -> 45.4 us (0.966)
  Pallas kernels: 46.2 us -> 44.6 us
    pallas_call x1, Pallas kernels: 43.8 us -> 43 us  [on_device(): pl.pallas_call(main_kernel, out_shape=(jax.ShapeDtypeStruct((rows, width)...]
    pallas_call x1, Pallas kernels: 2.39 us -> 1.62 us  [on_device(): pl.pallas_call(scale_kernel, out_shape=(jax.ShapeDtypeStruct((rows, width...]
where the time goes in v4:
time: 45.4 us; the launch traced here: 45.3 us
  Pallas kernels  44.6 us (98%)
  between operations  0.66 us (1%)
    pallas_call x1, Pallas kernels, on_device(): pl.pallas_call(main_kernel, out_shape=(jax.ShapeDtypeStruct((rows, width)...  43 us
    pallas_call x1, Pallas kernels, on_device(): pl.pallas_call(scale_kernel, out_shape=(jax.ShapeDtypeStruct((rows, width...  1.62 us

profile of v4, /device:TPU:1, one launch (start us, length us, event | category | flops | bytes accessed | tf_op | source)
XLA Modules:
  0.0 45.3 jit_solution(15531905053514403191)
XLA Ops:
  0.6 0.0 copy-start
  0.6 43.0 %main.1 = (bf16[512,2048]{1,0:T(8,128)(2,1)S(1)}, f32[4,16,128]{2,1,0:T(8,128)S(1)}, f32[8,2048]{1,0:T(8,128)S(1)}) custom-call(s32[4]{0:T(128)} %len_hbm.1, bf16[512,2048]{1,0:T(8,128)(2,1)} %q_hbm.1, bf16[512,2048]{1,0:T(8,128)(2,1)} %k_hbm.1, bf16[512,2048]{1,0:T(8,128)(2,1)} %v_hbm.1, bf16[512,2048]{1,0:T(8,128)(2,1)} %bitcast.4, ...), custom_call_target="tpu_custom_call" | custom-call | tf_op jit(solution)/shard_map/main/pallas_call | solution.py:365
  43.7 0.0 copy-done
  43.7 1.6 %scale.1 = (bf16[512,2048]{1,0:T(8,128)(2,1)}, bf16[2,4,2048]{2,1,0:T(4,128)(2,1)}) custom-call(bf16[512,2048]{1,0:T(8,128)(2,1)S(1)} %get-tuple-element.5.att, f32[4,16,128]{2,1,0:T(8,128)S(1)} %get-tuple-element.6.sums, f32[8,2048]{1,0:T(8,128)S(1)} %get-tuple-element.7.raw, f32[1,2048]{1,0:T(1,128)S(1)} %bitcast.3), custom_call_target="tpu_custom_call" | custom-call | tf_op jit(solution)/shard_map/scale/pallas_call | solution.py:418
Async XLA Ops:
  0.6 43.0 %copy-start = (f32[2048]{0:T(1024)S(1)}, f32[2048]{0:T(1024)}, u32[]{:S(2)}) copy-start(f32[2048]{0:T(1024)} %param.19) | copy-start | bytes 24580

commit v5 on v4

--- a/solution.py
+++ b/solution.py
@@ -86,7 +86,7 @@
             loads.append((tq_hbm, tq))
     loads += [(q_hbm, q), (len_hbm, len_ref), (tk_hbm, tk), (tv_hbm, tv), (sk_hbm, sk), (sv_hbm, sv)]
     loads = [pltpu.make_async_copy(src, dst, ld.at[n]) for n, (src, dst) in enumerate(loads)]
-    for copy in loads:
+    for copy in loads[:9]:
         copy.start()
 
     def send(src, dst, s, r, peer):
@@ -118,6 +118,8 @@
     loads[5].wait()
     loads[6].wait()
     lax.fori_loop(0, 4, my_state, 0, unroll=4)
+    for copy in loads[9:]:
+        copy.start()
     pl.semaphore_wait(barrier, len(peers))
     for i in range(NZ):
         send(xsend.at[i], xrecv.at[i], x_s, x_r, partner).start()

time: 45.4 us -> 45.4 us (level)
  no operation moved by 1% of the time
where the time goes in v5:
time: 45.4 us; the launch traced here: 45.3 us
  Pallas kernels  44.6 us (98%)
  between operations  0.66 us (1%)
    pallas_call x1, Pallas kernels, on_device(): pl.pallas_call(main_kernel, out_shape=(jax.ShapeDtypeStruct((rows, width)...  43 us
    pallas_call x1, Pallas kernels, on_device(): pl.pallas_call(scale_kernel, out_shape=(jax.ShapeDtypeStruct((rows, width...  1.62 us

profile of v5, /device:TPU:1, one launch (start us, length us, event | category | flops | bytes accessed | tf_op | source)
XLA Modules:
  0.0 45.3 jit_solution(4308769485250440536)
XLA Ops:
  0.6 0.0 copy-start
  0.6 43.0 %main.1 = (bf16[512,2048]{1,0:T(8,128)(2,1)S(1)}, f32[4,16,128]{2,1,0:T(8,128)S(1)}, f32[8,2048]{1,0:T(8,128)S(1)}) custom-call(s32[4]{0:T(128)} %len_hbm.1, bf16[512,2048]{1,0:T(8,128)(2,1)} %q_hbm.1, bf16[512,2048]{1,0:T(8,128)(2,1)} %k_hbm.1, bf16[512,2048]{1,0:T(8,128)(2,1)} %v_hbm.1, bf16[512,2048]{1,0:T(8,128)(2,1)} %bitcast.4, ...), custom_call_target="tpu_custom_call" | custom-call | tf_op jit(solution)/shard_map/main/pallas_call | solution.py:367
  43.7 0.0 copy-done
  43.7 1.6 %scale.1 = (bf16[512,2048]{1,0:T(8,128)(2,1)}, bf16[2,4,2048]{2,1,0:T(4,128)(2,1)}) custom-call(bf16[512,2048]{1,0:T(8,128)(2,1)S(1)} %get-tuple-element.5.att, f32[4,16,128]{2,1,0:T(8,128)S(1)} %get-tuple-element.6.sums, f32[8,2048]{1,0:T(8,128)S(1)} %get-tuple-element.7.raw, f32[1,2048]{1,0:T(1,128)S(1)} %bitcast.3), custom_call_target="tpu_custom_call" | custom-call | tf_op jit(solution)/shard_map/scale/pallas_call | solution.py:420
Async XLA Ops:
  0.6 43.0 %copy-start = (f32[2048]{0:T(1024)S(1)}, f32[2048]{0:T(1024)}, u32[]{:S(2)}) copy-start(f32[2048]{0:T(1024)} %param.19) | copy-start | bytes 24580
